TPU v7x, 32 devices: a whole 2x2x4 slice. The times are simulated.
32 devices in a mesh: section: 2 (over core), row: 4 (over z), col: 4 (over y, x).
Axes of the slice: x: 2, y: 2, z: 4, core: 2. Of those that a mesh axis runs over, the one named last changes fastest.
Arguments:
- queries: bfloat16 [16384, 4096], P(('section', 'col'), 'row'), may hold values from -8 to 8
- keys: bfloat16 [16384, 512], P(('section', 'col')), may hold values from -6 to 6
- values: bfloat16 [16384, 512], P(('section', 'col')), may hold values from -6 to 6
- out_grad: bfloat16 [16384, 4096], P(('section', 'col'), 'row'), may hold values from -12 to 12
- q_weight: bfloat16 [2048, 4096], P('col', 'row'), may hold values from -0.125 to 0.125
- k_weight: bfloat16 [2048, 512], P('col'), may hold values from -0.125 to 0.125
- v_weight: bfloat16 [2048, 512], P('col'), may hold values from -0.125 to 0.125
- resid_grad: bfloat16 [16384, 2048], P(('section', 'row', 'col')), may hold values from -4 to 4
- moe_input: bfloat16 [16384, 2048], P(('section', 'row', 'col')), may hold values from -6 to 6
- expert_ids: int32 [16384, 8], P(('section', 'row', 'col')), may hold values from 0 to 31, all different within a row; in each aligned block of 512 rows (0 to 511, 512 to 1023, ...) at most 144 rows name the same one
- route_weights: float32 [16384, 8], P(('section', 'row', 'col')), may hold values from 0.03 to 0.4
- w_gate_up: bfloat16 [32, 2048, 1536], P(('section', 'row', 'col')), may hold values from -0.125 to 0.125
- w_down: bfloat16 [32, 768, 2048], P(('section', 'row', 'col')), may hold values from -0.21875 to 0.21875
Outputs:
- moe_input_grad: bfloat16 [16384, 2048], P(('section', 'row', 'col'))
Inputs may be any that keep to these rules, and one draw needn't show every extreme that they name: `expert_ids`: each row names 8 different experts; among the rows of one device no expert is named by more than 144 rows, and in every draw some expert is named by exactly 144 rows of some device.
All inputs are finite; a program needn't handle non-finite values.
Results may differ from a plain program's by a relative error of at most 0.02.
Values may be sent and summed in bfloat16 or wider, within the bound.
A program may use at most 256 MiB of HBM per device.

v0:
```python
from functools import partial

import jax
import jax.numpy as jnp
from jax import lax
from jax.sharding import PartitionSpec as P

HEADS = 32
KV_HEADS = 4
HEAD_DIM = 128
TOPK = 8
DOC = 1024


def expert_math(rows_in, grad_in, w_gu, w_dn):
    width = w_dn.shape[0]
    gate_up = jnp.dot(rows_in, w_gu, preferred_element_type=jnp.float32)
    gate = gate_up[:, :width]
    up_part = gate_up[:, width:]
    dhidden = lax.dot_general(
        grad_in, w_dn, (((1,), (1,)), ((), ())), preferred_element_type=jnp.float32
    )
    sigm = jax.nn.sigmoid(gate)
    d_gate = dhidden * up_part * sigm * (1.0 + gate * (1.0 - sigm))
    d_up = dhidden * gate * sigm
    dgate_up = jnp.concatenate([d_gate, d_up], axis=1).astype(jnp.bfloat16)
    back_rows = lax.dot_general(
        dgate_up, w_gu, (((1,), (1,)), ((), ())), preferred_element_type=jnp.float32
    )
    return back_rows.astype(jnp.bfloat16)


def doc_backward(block, scale_val):
    query_blk, grad_blk, key_blk, value_blk = block
    doc_len = query_blk.shape[0]
    heads_here = query_blk.shape[1]
    causal = jnp.arange(doc_len)[:, None] >= jnp.arange(doc_len)[None, :]
    scores = (
        jnp.einsum("qhd,kd->hqk", query_blk, key_blk, preferred_element_type=jnp.float32)
        * scale_val
    )
    scores = jnp.where(causal[None], scores, -jnp.inf)
    top = jnp.max(scores, axis=-1, keepdims=True)
    expo = jnp.exp(scores - top)
    probs = expo / jnp.sum(expo, axis=-1, keepdims=True)
    probs_b = probs.astype(jnp.bfloat16)
    dprob = jnp.einsum("qhd,kd->hqk", grad_blk, value_blk, preferred_element_type=jnp.float32)
    delta = jnp.sum(probs * dprob, axis=-1, keepdims=True)
    dscore = (probs * (dprob - delta)).astype(jnp.bfloat16)
    dquery = (
        jnp.einsum("hqk,kd->qhd", dscore, key_blk, preferred_element_type=jnp.float32) * scale_val
    ).astype(jnp.bfloat16)
    dkey = (
        jnp.einsum("hqk,qhd->kd", dscore, query_blk, preferred_element_type=jnp.float32) * scale_val
    ).astype(jnp.bfloat16)
    dvalue = jnp.einsum(
        "hqk,qhd->kd", probs_b, grad_blk, preferred_element_type=jnp.float32
    ).astype(jnp.bfloat16)
    return jnp.concatenate(
        [dquery.reshape(doc_len, heads_here * key_blk.shape[1]), dkey, dvalue], axis=1
    )


def body(
    queries,
    keys,
    values,
    out_grad,
    q_weight,
    k_weight,
    v_weight,
    resid_grad,
    moe_input,
    expert_ids,
    route_weights,
    w_gate_up,
    w_down,
):
    row_count = lax.axis_size("row")
    heads_here = queries.shape[1] // HEAD_DIM
    group_size = HEADS // KV_HEADS
    kv_index = lax.axis_index("row") * heads_here // group_size
    key_head = lax.dynamic_slice_in_dim(keys, kv_index * HEAD_DIM, HEAD_DIM, 1)
    value_head = lax.dynamic_slice_in_dim(values, kv_index * HEAD_DIM, HEAD_DIM, 1)
    wk_local = lax.dynamic_slice_in_dim(k_weight, kv_index * HEAD_DIM, HEAD_DIM, 1)
    wv_local = lax.dynamic_slice_in_dim(v_weight, kv_index * HEAD_DIM, HEAD_DIM, 1)
    wcat_local = jnp.concatenate([q_weight, wk_local, wv_local], axis=1)
    wcat_whole = lax.all_gather(wcat_local, "col", axis=0, tiled=True)
    tok_rows = queries.shape[0]
    doc_count = tok_rows // DOC
    query_docs = queries.reshape(doc_count, DOC, heads_here, HEAD_DIM)
    grad_docs = out_grad.reshape(doc_count, DOC, heads_here, HEAD_DIM)
    key_docs = key_head.reshape(doc_count, DOC, HEAD_DIM)
    value_docs = value_head.reshape(doc_count, DOC, HEAD_DIM)
    dqkv = lax.map(
        partial(doc_backward, scale_val=HEAD_DIM ** (-0.5)),
        (query_docs, grad_docs, key_docs, value_docs),
    )
    dqkv = dqkv.reshape(tok_rows, dqkv.shape[-1])
    moe_rows = tok_rows // row_count
    term = lax.dot_general(
        dqkv, wcat_whole, (((1,), (1,)), ((), ())), preferred_element_type=jnp.float32
    )
    head_grad = lax.psum_scatter(
        lax.optimization_barrier(term.astype(jnp.bfloat16))
        .astype(jnp.float32)
        .astype(jnp.bfloat16),
        "row",
        scatter_dimension=0,
        tiled=True,
    ).astype(jnp.float32)
    layer_grad = head_grad + resid_grad.astype(jnp.float32)
    row_grad = layer_grad.astype(jnp.bfloat16)
    width = row_grad.shape[1]
    section_count = lax.axis_size("section")
    col_count = lax.axis_size("col")
    n_experts = section_count * row_count * col_count
    capacity = max(2, 9 * moe_rows * TOPK // (8 * n_experts))
    flat_ids = expert_ids.reshape(-1)
    onehot = (flat_ids[:, None] == jnp.arange(n_experts, dtype=jnp.int32)[None, :]).astype(
        jnp.int32
    )
    ranks = jnp.sum(jnp.cumsum(onehot, axis=0) * onehot, axis=1) - 1
    slots = flat_ids * capacity + ranks
    source = jnp.arange(moe_rows * TOPK, dtype=jnp.int32) // TOPK
    send_grads = (
        jnp.zeros((n_experts * capacity, width), jnp.bfloat16).at[slots].set(row_grad[source])
    )
    send_rows = (
        jnp.zeros((n_experts * capacity, width), jnp.bfloat16).at[slots].set(moe_input[source])
    )
    w_gu = w_gate_up[0]
    w_dn = w_down[0]
    grads_in = lax.all_to_all(
        send_grads.reshape(n_experts, capacity, width),
        ("section", "row", "col"),
        split_axis=0,
        concat_axis=0,
        tiled=True,
    )
    lead = grads_in.shape[:-1]
    result = expert_math(
        lax.all_to_all(
            send_rows.reshape(n_experts, capacity, width),
            ("section", "row", "col"),
            split_axis=0,
            concat_axis=0,
            tiled=True,
        ).reshape(-1, width),
        grads_in.reshape(-1, width),
        w_gu,
        w_dn,
    )
    result = result.reshape(lead + (width,))
    returned = lax.all_to_all(
        result, ("section", "row", "col"), split_axis=0, concat_axis=0, tiled=True
    )
    returned = returned.reshape(n_experts * capacity, width)
    pair_rows = returned[slots].astype(jnp.float32).reshape(moe_rows, TOPK, width)
    combined = jnp.sum(pair_rows * route_weights[:, :, None], axis=1)
    return combined.astype(jnp.bfloat16)


def solution(mesh):
    return jax.shard_map(
        body,
        mesh=mesh,
        in_specs=(
            P(("section", "col"), "row"),
            P(("section", "col"), None),
            P(("section", "col"), None),
            P(("section", "col"), "row"),
            P("col", "row"),
            P("col", None),
            P("col", None),
            P(("section", "row", "col"), None),
            P(("section", "row", "col"), None),
            P(("section", "row", "col"), None),
            P(("section", "row", "col"), None),
            P(("section", "row", "col"), None, None),
            P(("section", "row", "col"), None, None),
        ),
        out_specs=P(("section", "row", "col"), None),
        check_vma=False,
    )
```

profile of v0, /device:TPU:0, one launch (start us, length us, event | category | flops | bytes accessed | tf_op | source)
XLA Modules:
  0.0 1720.9 jit_solution(1937897511863305296)
XLA Ops:
  6.5 0.0 copy-start
  6.5 1.1 constant_dynamic-slice_fusion.2
  7.7 2.5 pad_maximum_fusion
  10.2 0.0 all-gather.2.cloned.1.call-update
  10.2 0.8 copy.28
  11.1 0.1 eq.29
  11.2 0.1 eq.25
  11.4 0.7 broadcast_multiply_fusion
  12.1 0.9 fusion.62
  13.0 18.1 %reduce-window.6 = s32[32,32,128]{2,1,0:T(8,128)} reduce-window(s32[32,32,128]{2,1,0:T(8,128)} %fusion.62, s32[]{:T(128)} %copy.93), window={size=1x1x128 pad=0_0x0_0x127_0}, to_apply=%region_0.1 | reduce-window | flops 16646144 | bytes 1048580 | tf_op jit(solution)/shard_map/reduce-window
  31.0 1.8 slice_reduce_fusion
  32.8 0.2 reduce-window.9
  33.0 1.2 broadcast_add_fusion
  34.3 0.3 fusion.61
  34.6 0.1 copy.27
  34.8 0.2 mul.75
  35.0 33.2 %gather_fusion.1 = bf16[4096,2048]{1,0:T(8,128)(2,1)} fusion(bf16[512,2048]{1,0:T(8,128)(2,1)} %param.23, s32[4096]{0:T(1024)S(1)} %broadcast_clamp_fusion.1), kind=kCustom, calls=%fused_computation.1 | custom fusion | bytes 33570816 | tf_op jit(solution)/shard_map/gather | solution.py:130
  68.2 34.8 %scatter_custom_fusion.1 = bf16[4608,2048]{1,0:T(8,128)(2,1)} fusion(s32[4096]{0:T(1024)S(1)} %bitcast.181, bf16[4096,2048]{1,0:T(8,128)(2,1)} %gather_fusion.1, bf16[]{:T(256)} %constant.63.clone.1), kind=kCustom, calls=%fused_computation.63 | custom fusion | bytes 18874880 | tf_op jit(solution)/shard_map/scatter | solution.py:130
  103.0 7.4 all-to-all-start.1
  110.4 0.0 reduce-scatter.2.cloned.1.call-start
  110.5 5.3 copy.46
  115.7 5.3 copy.47
  121.1 2.3 constant_dynamic-slice_fusion.4
  123.3 264.8 %while.10 = (s32[]{:T(128)}, bf16[2,1024,1280]{2,1,0:T(8,128)(2,1)}, bf16[2,1024,128]{2,1,0:T(8,128)(2,1)}, bf16[2,1024,8,128]{3,2,1,0:T(8,128)(2,1)}, bf16[2,10...) while((s32[]{:T(128)}, bf16[2,1024,1280]{2,1,0:T(8,128)(2,1)}, ...), condition=%wide.region_7.8_spmd, body=%wide.region_3.7_spmd.sunk | while | flops 10857866240 | bytes 289867840 | solution.py:95
  135.8 4.5 constant_dynamic-slice_fusion.7
  140.3 1.3 iota_compare_fusion.4
  141.6 19.1 %fusion.90 = (f32[8,1024]{1,0:T(8,128)S(1)}, f32[8,1024,1024]{1,2,0:T(8,128)}) fusion(pred[1024,1024]{0,1:T(8,128)(4,1)} %iota_compare_fusion.4, bf16[1,1024,8,128]{3,2,1,0:T(8,128)(2,1)} %get-tuple-element.112, bf16[2,1024,128]{2,1,0:T(8,128)(2,1)} %get-tuple-element.133, s32[]{:T(128)} %get-tuple-element.124), kind=kOutput, calls=%fused_computation.98.clone.1 | convolution fusion | flops 2181039104 | bytes 36995584 | tf_op jit(solution)/shard_map/while/body/eval_jaxpr/sub | solution.py:44
  160.7 25.3 %fusion.92 = (f32[8,1024]{1,0:T(8,128)S(1)}, f32[1024,1024,8]{1,0,2:T(8,128)}) fusion(f32[8,1024,1024]{1,2,0:T(8,128)} %get-tuple-element.113, f32[8,1024]{1,0:T(8,128)S(1)} %get-tuple-element.114, bf16[1,1024,8,128]{3,2,1,0:T(8,128)(2,1)} %get-tuple-element.111, bf16[2,1024,128]{2,1,0:T(8,128)(2,1)} %get-tuple-element.135, s32[]{:T(128)} %get-tuple-element.124), kind=kOutput, calls=%fused_computation.8.clone.1 | convolution fusion | flops 2172641280 | bytes 69534208 | tf_op jit(solution)/shard_map/while/body/eval_jaxpr/qhd,kd->hqk/dot_general | solution.py:47
  186.0 28.0 %fusion.93 = bf16[8,1024,1024]{1,2,0:T(8,128)(2,1)} fusion(f32[1024,1024,8]{1,0,2:T(8,128)} %get-tuple-element.115, f32[8,1024]{1,0:T(8,128)S(1)} %get-tuple-element.116, f32[8,1024,1024]{1,2,0:T(8,128)} %get-tuple-element.113, f32[8,1024]{1,0:T(8,128)S(1)} %get-tuple-element.114), kind=kLoop, calls=%fused_computation.10.clone.1 | loop fusion | flops 33554432 | bytes 83951616 | tf_op jit(solution)/shard_map/while/body/eval_jaxpr/convert_element_type | solution.py:49
  214.0 9.8 multiply_convert_fusion.3
  223.8 12.0 fusion.94
  235.8 14.8 fusion.91
  250.6 3.4 maximum_bitcast_fusion.2
  254.0 4.4 copy.85
  258.4 3.4 constant_dynamic-update-slice_fusion.2
  261.8 4.5 constant_dynamic-slice_fusion.7
  266.3 1.3 iota_compare_fusion.4
  267.6 19.1 %fusion.90 = (f32[8,1024]{1,0:T(8,128)S(1)}, f32[8,1024,1024]{1,2,0:T(8,128)}) fusion(pred[1024,1024]{0,1:T(8,128)(4,1)} %iota_compare_fusion.4, bf16[1,1024,8,128]{3,2,1,0:T(8,128)(2,1)} %get-tuple-element.112, bf16[2,1024,128]{2,1,0:T(8,128)(2,1)} %get-tuple-element.133, s32[]{:T(128)} %get-tuple-element.124), kind=kOutput, calls=%fused_computation.98.clone.1 | convolution fusion | flops 2181039104 | bytes 36995584 | tf_op jit(solution)/shard_map/while/body/eval_jaxpr/sub | solution.py:44
  286.6 25.3 %fusion.92 = (f32[8,1024]{1,0:T(8,128)S(1)}, f32[1024,1024,8]{1,0,2:T(8,128)}) fusion(f32[8,1024,1024]{1,2,0:T(8,128)} %get-tuple-element.113, f32[8,1024]{1,0:T(8,128)S(1)} %get-tuple-element.114, bf16[1,1024,8,128]{3,2,1,0:T(8,128)(2,1)} %get-tuple-element.111, bf16[2,1024,128]{2,1,0:T(8,128)(2,1)} %get-tuple-element.135, s32[]{:T(128)} %get-tuple-element.124), kind=kOutput, calls=%fused_computation.8.clone.1 | convolution fusion | flops 2172641280 | bytes 69534208 | tf_op jit(solution)/shard_map/while/body/eval_jaxpr/qhd,kd->hqk/dot_general | solution.py:47
  311.9 28.0 %fusion.93 = bf16[8,1024,1024]{1,2,0:T(8,128)(2,1)} fusion(f32[1024,1024,8]{1,0,2:T(8,128)} %get-tuple-element.115, f32[8,1024]{1,0:T(8,128)S(1)} %get-tuple-element.116, f32[8,1024,1024]{1,2,0:T(8,128)} %get-tuple-element.113, f32[8,1024]{1,0:T(8,128)S(1)} %get-tuple-element.114), kind=kLoop, calls=%fused_computation.10.clone.1 | loop fusion | flops 33554432 | bytes 83951616 | tf_op jit(solution)/shard_map/while/body/eval_jaxpr/convert_element_type | solution.py:49
  339.9 9.8 multiply_convert_fusion.3
  349.7 12.0 fusion.94
  361.7 14.8 fusion.91
  376.5 3.4 maximum_bitcast_fusion.2
  379.9 4.4 copy.85
  384.3 3.5 constant_dynamic-update-slice_fusion.2
  388.1 0.0 all-gather.2.cloned.1.call-done
  388.2 16.7 convolution_convert_fusion.1
  404.9 0.0 reduce-scatter.2.cloned.1.call-update
  404.9 236.7 %reduce-scatter.2.cloned.1.call-done = bf16[512,2048]{1,0:T(8,128)(2,1)} async-done(((bf16[2048,2048]{1,0:T(8,128)(2,1)}), bf16[512,2048]{1,0:T(8,128)(2,1)}) %reduce-scatter.2.cloned.1.call-update) | async-done | bytes 2097168 | tf_op jit(solution)/shard_map/reduce_scatter | solution.py:104
  641.6 4.4 add_convert_fusion
  646.0 33.2 %gather_fusion = bf16[4096,2048]{1,0:T(8,128)(2,1)} fusion(bf16[512,2048]{1,0:T(8,128)(2,1)} %add_convert_fusion, s32[4096]{0:T(1024)S(1)} %copy-done.2), kind=kCustom, calls=%fused_computation | custom fusion | bytes 33570816 | tf_op jit(solution)/shard_map/gather | solution.py:127
  679.2 34.8 %scatter_custom_fusion = bf16[4608,2048]{1,0:T(8,128)(2,1)} fusion(s32[4096]{0:T(1024)} %bitcast.182, bf16[4096,2048]{1,0:T(8,128)(2,1)} %gather_fusion, bf16[]{:T(256)} %constant.63.clone.1), kind=kCustom, calls=%fused_computation.65 | custom fusion | bytes 18874880 | tf_op jit(solution)/shard_map/scatter | solution.py:127
  714.0 0.0 all-to-all-done.1
  714.0 27.5 %all-to-all-start = ((bf16[32,144,2048]{2,1,0:T(8,128)(2,1)}), bf16[32,144,2048]{2,1,0:T(8,128)(2,1)}, u32[]{:S(2)}, u32[]{:S(2)}) async-start(bf16[32,144,2048]{2,1,0:T(8,128)(2,1)} %bitcast.171), calls=%async_computation.1 | async-start | bytes 37748736 | tf_op jit(solution)/shard_map/all_to_all | solution.py:134
  741.5 36.7 %fusion.56 = f32[4608,1536]{0,1:T(8,128)} fusion(bf16[4608,2048]{1,0:T(8,128)(2,1)} %bitcast.25, bf16[1,2048,1536]{2,1,0:T(8,128)(2,1)} %param.26), kind=kOutput, calls=%fused_computation.69 | convolution fusion | flops 28991029248 | bytes 53477376 | tf_op jit(solution)/shard_map/dot_general | solution.py:17
  778.2 382.9 %all-to-all-done = bf16[32,144,2048]{2,1,0:T(8,128)(2,1)} async-done(((bf16[32,144,2048]{2,1,0:T(8,128)(2,1)}), bf16[32,144,2048]{2,1,0:T(8,128)(2,1)}, u32[]{:S(2)}, u32[]{:S(2)}) %all-to-all-start) | async-done | bytes 18874400 | tf_op jit(solution)/shard_map/all_to_all | solution.py:134
  1161.1 30.9 %fusion.47 = (bf16[4608,768]{0,1:T(8,128)(2,1)}, bf16[4608,768]{0,1:T(8,128)(2,1)}) fusion(f32[4608,1536]{0,1:T(8,128)} %fusion.56, bf16[4608,2048]{1,0:T(8,128)(2,1)} %bitcast.22, bf16[1,768,2048]{2,1,0:T(8,128)(2,1)S(1)} %copy-done), kind=kOutput, calls=%fused_computation.57 | convolution fusion | flops 14541520896 | bytes 64487424 | tf_op jit(solution)/shard_map/dot_general | solution.py:20
  1192.0 36.6 %convolution_convert_fusion = bf16[4608,2048]{1,0:T(8,128)(2,1)} fusion(bf16[4608,768]{0,1:T(8,128)(2,1)} %get-tuple-element.63, bf16[4608,768]{0,1:T(8,128)(2,1)} %get-tuple-element.62, bf16[1,2048,1536]{2,1,0:T(8,128)(2,1)} %param.26), kind=kOutput, calls=%fused_computation.53 | convolution fusion | flops 29028777984 | bytes 39321600 | tf_op jit(solution)/shard_map/dot_general | solution.py:27
  1228.7 8.8 all-to-all-start.2
  1237.5 0.1 copy.33
  1237.7 419.4 %all-to-all-done.2 = bf16[32,144,2048]{2,1,0:T(8,128)(2,1)} async-done(((bf16[32,144,2048]{2,1,0:T(8,128)(2,1)}), bf16[32,144,2048]{2,1,0:T(8,128)(2,1)}, u32[]{:S(2)}, u32[]{:S(2)}) %all-to-all-start.2) | async-done | bytes 18874400 | tf_op jit(solution)/shard_map/all_to_all | solution.py:155
  1657.1 40.1 %gather_fusion.2 = bf16[4096,2048]{1,0:T(8,128)(2,1)} fusion(bf16[4608,2048]{1,0:T(8,128)(2,1)} %bitcast.28, s32[4096]{0:T(1024)S(1)} %broadcast_clamp_fusion), kind=kCustom, calls=%fused_computation.2 | custom fusion | bytes 33570816 | tf_op jit(solution)/shard_map/gather | solution.py:159
  1697.2 16.3 fusion.44
  (18 shorter events, 0.1 us)
Async XLA Ops:
  6.5 1154.6 %copy-start = (bf16[1,768,2048]{2,1,0:T(8,128)(2,1)S(1)}, bf16[1,768,2048]{2,1,0:T(8,128)(2,1)}, u32[]{:S(2)}) copy-start(bf16[1,768,2048]{2,1,0:T(8,128)(2,1)} %param.27) | copy-start | bytes 9437188
  6.5 381.6 %all-gather.2.cloned.1.call-start = ((), (), s32[]{:S(2)}) async-start(), calls=%async_computation.4 | async-start | bytes 6553600 | tf_op jit(solution)/shard_map/all_gather | solution.py:88
  12.1 56.1 %copy-start.1 = (s32[4096]{0:T(1024)}, s32[4096]{0:T(1024)S(1)}, u32[]{:S(2)}) copy-start(s32[4096]{0:T(1024)S(1)} %broadcast_clamp_fusion.1) | copy-start | bytes 49156
  35.0 33.2 %copy-start.3 = (s32[4096,1]{0,1:T(1,128)}, s32[4096,1]{0,1:T(1,128)S(1)}, u32[]{:S(2)}) copy-start(s32[4096,1]{0,1:T(1,128)S(1)} %compare_select_fusion.1) | copy-start | bytes 49156
  103.0 611.0 %all-to-all-start.1 = ((bf16[32,144,2048]{2,1,0:T(8,128)(2,1)}), bf16[32,144,2048]{2,1,0:T(8,128)(2,1)}, u32[]{:S(2)}, u32[]{:S(2)}) async-start(bf16[32,144,2048]{2,1,0:T(8,128)(2,1)} %bitcast.170), calls=%async_computation.2 | async-start | bytes 37748736 | tf_op jit(solution)/shard_map/all_to_all | solution.py:143
  110.4 531.1 %reduce-scatter.2.cloned.1.call-start = ((), (), s32[]{:S(2)}) async-start(), calls=%async_computation.5 | async-start | bytes 10485760 | tf_op jit(solution)/shard_map/reduce_scatter | solution.py:104
  404.9 241.2 %copy-start.2 = (s32[4096]{0:T(1024)S(1)}, s32[4096]{0:T(1024)}, u32[]{:S(2)}) copy-start(s32[4096]{0:T(1024)} %copy-done.1) | copy-start | bytes 49156
  714.0 447.1 %all-to-all-start = ((bf16[32,144,2048]{2,1,0:T(8,128)(2,1)}), bf16[32,144,2048]{2,1,0:T(8,128)(2,1)}, u32[]{:S(2)}, u32[]{:S(2)}) async-start(bf16[32,144,2048]{2,1,0:T(8,128)(2,1)} %bitcast.171), calls=%async_computation.1 | async-start | bytes 37748736 | tf_op jit(solution)/shard_map/all_to_all | solution.py:134
  1228.7 8.8 copy-start.5
  1228.7 9.0 copy-start.4
  1228.7 428.4 %all-to-all-start.2 = ((bf16[32,144,2048]{2,1,0:T(8,128)(2,1)}), bf16[32,144,2048]{2,1,0:T(8,128)(2,1)}, u32[]{:S(2)}, u32[]{:S(2)}) async-start(bf16[32,144,2048]{2,1,0:T(8,128)(2,1)} %bitcast.174), calls=%async_computation.3 | async-start | bytes 37748736 | tf_op jit(solution)/shard_map/all_to_all | solution.py:155
Sparse Core Ops, SparseCore 0:
  10.3 64.0 all-gather.1
  405.0 236.5 reduce-scatter.1
where the time goes:
time: 1730 us; the launch traced here: 1720 us
  waiting for transfers between devices  1040 us (60%)
  matrix products  283 us (16%)
  local copies, waits for them, and re-layouts  218 us (13%)
  other arithmetic  110 us (6%)
  starting transfers between devices  43.8 us (3%)
    all_to_all x1, waiting for transfers between devices, body(): lax.all_to_all(result, ('section', 'row', 'col'), split_axis=0, concat_ax...  419 us
    all_to_all x1, waiting for transfers between devices, body(): lax.all_to_all(send_grads.reshape(n_experts, capacity, width), ('section'...  383 us
    reduce_scatter x1, waiting for transfers between devices, body(): lax.psum_scatter(lax.optimization_barrier(term.astype(jnp.bfloat16)).asty...  237 us
    scatter x2, local copies, waits for them, and re-layouts, body(): jnp.zeros((n_experts * capacity, width), jnp.bfloat16).at[slots]  69.5 us
    convert_element_type x2, other arithmetic, doc_backward(): dscore = (probs * (dprob - delta)).astype(jnp.bfloat16)  55.9 us
    dot_general x2, matrix products, doc_backward(): jnp.einsum('qhd,kd->hqk', grad_blk, value_blk, preferred_element_type=jnp...  50.6 us
    gather x1, local copies, waits for them, and re-layouts, body(): returned[slots].astype(jnp.float32).reshape(moe_rows, TOPK, width)  40.1 us
    sub x2, matrix products, doc_backward(): expo = jnp.exp(scores - top)  38.1 us
  transfers between devices with their start and end apart: 5, of which 3 were waited for; matrix products, arithmetic and copies ran while one was open for 28% of the time, Pallas kernels for 0%

commit v1 on v0

v1 whole, which is shorter than its diff:
```python
from functools import partial

import jax
import jax.numpy as jnp
from jax import lax
from jax.experimental import pallas as pl
from jax.experimental.pallas import tpu as pltpu
from jax.sharding import PartitionSpec as P

HEADS = 32
KV_HEADS = 4
HEAD_DIM = 128
TOPK = 8
DOC = 1024
CHUNKS = 2


def pick_kernel(pos_ref, rows_ref, out_ref):
    cap = out_ref.shape[2]
    tokens = rows_ref.shape[1]
    pos = pos_ref[0, 0]
    slot = lax.broadcasted_iota(jnp.int32, (cap, tokens), 0)
    onehot = jnp.where(slot == pos, 1.0, 0.0).astype(jnp.bfloat16)
    picked = jnp.dot(onehot, rows_ref[0], preferred_element_type=jnp.float32)
    out_ref[0, 0] = picked.astype(out_ref.dtype)


def pick_rows(pos, rows, cap):
    peers, groups, _, tokens = pos.shape
    width = rows.shape[2]
    return pl.pallas_call(
        pick_kernel,
        grid=(groups, peers),
        in_specs=[
            pl.BlockSpec((1, 1, 1, tokens), lambda g, p: (p, g, 0, 0)),
            pl.BlockSpec((1, tokens, width), lambda g, p: (g, 0, 0)),
        ],
        out_specs=pl.BlockSpec((1, 1, cap, width), lambda g, p: (p, g, 0, 0)),
        out_shape=jax.ShapeDtypeStruct((peers, groups, cap, width), rows.dtype),
        cost_estimate=pl.CostEstimate(
            flops=2 * peers * groups * cap * tokens * width,
            bytes_accessed=2 * width * groups * (tokens + peers * cap),
            transcendentals=0,
        ),
        name="pick_rows",
    )(pos, rows)


def mix_kernel(pos_ref, weight_ref, rows_ref, out_ref, total_ref):
    peer = pl.program_id(1)
    cap = rows_ref.shape[2]
    tokens = out_ref.shape[0]
    slot = lax.broadcasted_iota(jnp.int32, (cap, tokens), 0)
    spread = jnp.where(slot == pos_ref[0, 0], weight_ref[0, 0], 0.0).astype(jnp.bfloat16)
    term = lax.dot_general(
        spread, rows_ref[0, 0], (((0,), (0,)), ((), ())), preferred_element_type=jnp.float32
    )

    @pl.when(peer == 0)
    def _():
        total_ref[...] = term

    @pl.when(peer > 0)
    def _():
        total_ref[...] += term

    @pl.when(peer == pl.num_programs(1) - 1)
    def _():
        out_ref[...] = total_ref[...].astype(out_ref.dtype)


def mix_rows(pos, weight, rows):
    peers, groups, _, tokens = pos.shape
    cap, width = rows.shape[2:]
    return pl.pallas_call(
        mix_kernel,
        grid=(groups, peers),
        in_specs=[
            pl.BlockSpec((1, 1, 1, tokens), lambda g, p: (p, g, 0, 0)),
            pl.BlockSpec((1, 1, 1, tokens), lambda g, p: (p, g, 0, 0)),
            pl.BlockSpec((1, 1, cap, width), lambda g, p: (p, g, 0, 0)),
        ],
        out_specs=pl.BlockSpec((tokens, width), lambda g, p: (g, 0)),
        out_shape=jax.ShapeDtypeStruct((groups * tokens, width), rows.dtype),
        scratch_shapes=[pltpu.VMEM((tokens, width), jnp.float32)],
        cost_estimate=pl.CostEstimate(
            flops=2 * peers * groups * cap * tokens * width,
            bytes_accessed=2 * width * groups * (tokens + peers * cap),
            transcendentals=0,
        ),
        name="mix_rows",
    )(pos, weight, rows)


def doc_backward(block, scale_val):
    query_blk, grad_blk, key_blk, value_blk = block
    doc_len = query_blk.shape[0]
    heads_here = query_blk.shape[1]
    causal = jnp.arange(doc_len)[:, None] >= jnp.arange(doc_len)[None, :]
    scores = (
        jnp.einsum("qhd,kd->hqk", query_blk, key_blk, preferred_element_type=jnp.float32)
        * scale_val
    )
    scores = jnp.where(causal[None], scores, -jnp.inf)
    top = jnp.max(scores, axis=-1, keepdims=True)
    expo = jnp.exp(scores - top)
    probs = expo / jnp.sum(expo, axis=-1, keepdims=True)
    probs_b = probs.astype(jnp.bfloat16)
    dprob = jnp.einsum("qhd,kd->hqk", grad_blk, value_blk, preferred_element_type=jnp.float32)
    delta = jnp.sum(probs * dprob, axis=-1, keepdims=True)
    dscore = (probs * (dprob - delta)).astype(jnp.bfloat16)
    dquery = (
        jnp.einsum("hqk,kd->qhd", dscore, key_blk, preferred_element_type=jnp.float32) * scale_val
    ).astype(jnp.bfloat16)
    dkey = (
        jnp.einsum("hqk,qhd->kd", dscore, query_blk, preferred_element_type=jnp.float32) * scale_val
    ).astype(jnp.bfloat16)
    dvalue = jnp.einsum(
        "hqk,qhd->kd", probs_b, grad_blk, preferred_element_type=jnp.float32
    ).astype(jnp.bfloat16)
    return jnp.concatenate(
        [dquery.reshape(doc_len, heads_here * key_blk.shape[1]), dkey, dvalue], axis=1
    )


def body(
    queries,
    keys,
    values,
    out_grad,
    q_weight,
    k_weight,
    v_weight,
    resid_grad,
    moe_input,
    expert_ids,
    route_weights,
    w_gate_up,
    w_down,
):
    row_count = lax.axis_size("row")
    heads_here = queries.shape[1] // HEAD_DIM
    group_size = HEADS // KV_HEADS
    kv_index = lax.axis_index("row") * heads_here // group_size
    key_head = lax.dynamic_slice_in_dim(keys, kv_index * HEAD_DIM, HEAD_DIM, 1)
    value_head = lax.dynamic_slice_in_dim(values, kv_index * HEAD_DIM, HEAD_DIM, 1)
    wk_local = lax.dynamic_slice_in_dim(k_weight, kv_index * HEAD_DIM, HEAD_DIM, 1)
    wv_local = lax.dynamic_slice_in_dim(v_weight, kv_index * HEAD_DIM, HEAD_DIM, 1)
    wcat_local = jnp.concatenate([q_weight, wk_local, wv_local], axis=1)
    wcat_whole = lax.all_gather(wcat_local, "col", axis=0, tiled=True)
    section_count = lax.axis_size("section")
    col_count = lax.axis_size("col")
    peers = section_count * col_count
    n_experts = peers * row_count
    tok_rows = queries.shape[0]
    moe_rows = tok_rows // row_count
    model = q_weight.shape[0] * col_count
    capacity = max(2, 9 * moe_rows * TOPK // (8 * n_experts))

    ids_line = lax.all_gather(expert_ids, "row", axis=0, tiled=False)
    weights_line = lax.all_gather(route_weights, "row", axis=0, tiled=False)
    rows_line = lax.all_gather(moe_input, "row", axis=0, tiled=False)
    peer = jnp.arange(peers, dtype=jnp.int32)
    peer_expert = (
        (peer // col_count) * row_count + lax.axis_index("row")
    ) * col_count + peer % col_count
    named = ids_line[None] == peer_expert[:, None, None, None]
    hit = jnp.any(named, axis=-1)
    weight = jnp.sum(jnp.where(named, weights_line[None], 0.0), axis=-1)
    order = jnp.arange(moe_rows, dtype=jnp.int32)
    before = (order[:, None] < order[None, :]).astype(jnp.bfloat16)
    rank = lax.dot_general(
        hit.astype(jnp.bfloat16).reshape(peers * row_count, moe_rows),
        before,
        (((1,), (0,)), ((), ())),
        preferred_element_type=jnp.float32,
    ).reshape(peers, row_count, moe_rows)
    pos = jnp.where(hit, rank.astype(jnp.int32), -1)[:, :, None, :]
    weight = weight[:, :, None, :]

    def swap(blocks):
        return lax.all_to_all(
            blocks, ("section", "col"), split_axis=0, concat_axis=0, tiled=True
        )

    w_gu = w_gate_up[0]
    w_dn = w_down[0]
    ff = w_dn.shape[0]
    rows_in = swap(pick_rows(pos, rows_line, capacity)).reshape(-1, model)
    gate_up = jnp.dot(rows_in, w_gu, preferred_element_type=jnp.float32)

    doc_count = tok_rows // DOC
    query_docs = queries.reshape(doc_count, DOC, heads_here, HEAD_DIM)
    grad_docs = out_grad.reshape(doc_count, DOC, heads_here, HEAD_DIM)
    key_docs = key_head.reshape(doc_count, DOC, HEAD_DIM)
    value_docs = value_head.reshape(doc_count, DOC, HEAD_DIM)
    dqkv = lax.map(
        partial(doc_backward, scale_val=HEAD_DIM ** (-0.5)),
        (query_docs, grad_docs, key_docs, value_docs),
    )
    dqkv = dqkv.reshape(tok_rows, dqkv.shape[-1])

    span = model // CHUNKS
    dhidden = None
    for chunk in range(CHUNKS):
        lo, hi = chunk * span, (chunk + 1) * span
        term = lax.dot_general(
            dqkv,
            wcat_whole[lo:hi],
            (((1,), (1,)), ((), ())),
            preferred_element_type=jnp.float32,
        )
        head_grad = lax.psum_scatter(
            term.astype(jnp.bfloat16), "row", scatter_dimension=0, tiled=True
        ).astype(jnp.float32)
        layer_grad = head_grad + resid_grad[:, lo:hi].astype(jnp.float32)
        row_grad = layer_grad.astype(jnp.bfloat16)
        grads_line = lax.all_gather(row_grad, "row", axis=0, tiled=False)
        grads_in = swap(pick_rows(pos, grads_line, capacity)).reshape(-1, span)
        piece = lax.dot_general(
            grads_in,
            w_dn[:, lo:hi],
            (((1,), (1,)), ((), ())),
            preferred_element_type=jnp.float32,
        )
        dhidden = piece if dhidden is None else dhidden + piece

    gate = gate_up[:, :ff]
    up_part = gate_up[:, ff:]
    sigm = jax.nn.sigmoid(gate)
    d_gate = dhidden * up_part * sigm * (1.0 + gate * (1.0 - sigm))
    d_up = dhidden * gate * sigm
    dgate_up = jnp.concatenate([d_gate, d_up], axis=1).astype(jnp.bfloat16)

    pieces = []
    for chunk in range(CHUNKS):
        lo, hi = chunk * span, (chunk + 1) * span
        back_rows = lax.dot_general(
            dgate_up,
            w_gu[lo:hi],
            (((1,), (1,)), ((), ())),
            preferred_element_type=jnp.float32,
        ).astype(jnp.bfloat16)
        returned = swap(back_rows.reshape(peers, row_count, capacity, span))
        mixed = mix_rows(pos, weight, returned)
        pieces.append(lax.psum_scatter(mixed, "row", scatter_dimension=0, tiled=True))
    return jnp.concatenate(pieces, axis=1)


def solution(mesh):
    return jax.shard_map(
        body,
        mesh=mesh,
        in_specs=(
            P(("section", "col"), "row"),
            P(("section", "col"), None),
            P(("section", "col"), None),
            P(("section", "col"), "row"),
            P("col", "row"),
            P("col", None),
            P("col", None),
            P(("section", "row", "col"), None),
            P(("section", "row", "col"), None),
            P(("section", "row", "col"), None),
            P(("section", "row", "col"), None),
            P(("section", "row", "col"), None, None),
            P(("section", "row", "col"), None, None),
        ),
        out_specs=P(("section", "row", "col"), None),
        check_vma=False,
    )
```

time: 1730 us -> 1150 us (0.66)
  waiting for transfers between devices: 1040 us -> 536 us
  local copies, waits for them, and re-layouts: 218 us -> 34.1 us
  Pallas kernels: 0 us -> 130 us
  other arithmetic: 110 us -> 71.8 us
  blocking collectives: 0 us -> 28.7 us
    all_to_all x3 -> x5, waiting for transfers between devices: 802 us -> 200 us  [swap(): lax.all_to_all(blocks, ('section', 'col'), split_axis=0, concat_axis=0, t...]
    all_gather x0 -> x3, waiting for transfers between devices: none -> 163 us  [the longest x2 163 us: body(): grads_line = lax.all_gather(row_grad, 'row', axis=0, tiled=False)]
    pallas_call x0 -> x5, Pallas kernels: none -> 130 us  [the longest x3 70.1 us: pick_rows(): pl.pallas_call(pick_kernel, grid=(groups, peers), in_specs=[pl.BlockSpec(...]
    gather x3 -> x0, local copies, waits for them, and re-layouts: 106 us -> none  [the longest x1 40.1 us: body(): returned[slots].astype(jnp.float32).reshape(moe_rows, TOPK, width)]
    scatter x2 -> x0, local copies, waits for them, and re-layouts: 69.5 us -> none  [body(): jnp.zeros((n_experts * capacity, width), jnp.bfloat16).at[slots]]
    reduce_scatter x1 -> x4, waiting for transfers between devices: 237 us -> 172 us  [the longest x2 98.2 us: body(): lax.psum_scatter(term.astype(jnp.bfloat16), 'row', scatter_dimension=0, t...]
    all_gather x0 -> x2, blocking collectives: none -> 28.7 us  [the longest x1 15.5 us: body(): ids_line = lax.all_gather(expert_ids, 'row', axis=0, tiled=False)]
    another operation x3 -> x0, other arithmetic: 19.5 us -> none
  transfers between devices with their start and end apart: 5 -> 13, of which waited for: 3 -> 9; matrix products, arithmetic and copies ran while one was open for 28% -> 31% of each run, Pallas kernels for 0% -> 11%
where the time goes in v1:
time: 1150 us; the launch traced here: 1140 us
  waiting for transfers between devices  536 us (47%)
  matrix products  300 us (26%)
  Pallas kernels  130 us (11%)
  other arithmetic  71.8 us (6%)
  local copies, waits for them, and re-layouts  34.1 us (3%)
  blocking collectives  28.7 us (2%)
  starting transfers between devices  26.8 us (2%)
  between operations  13.9 us (1%)
    all_to_all x5, waiting for transfers between devices, swap(): lax.all_to_all(blocks, ('section', 'col'), split_axis=0, concat_axis=0, t...  200 us
    all_gather x2, waiting for transfers between devices, body(): grads_line = lax.all_gather(row_grad, 'row', axis=0, tiled=False)  163 us
    reduce_scatter x2, waiting for transfers between devices, body(): lax.psum_scatter(term.astype(jnp.bfloat16), 'row', scatter_dimension=0, t...  98.2 us
    reduce_scatter x2, waiting for transfers between devices, body(): lax.psum_scatter(mixed, 'row', scatter_dimension=0, tiled=True)  74.2 us
    pallas_call x3, Pallas kernels, pick_rows(): pl.pallas_call(pick_kernel, grid=(groups, peers), in_specs=[pl.BlockSpec(...  70.1 us
    pallas_call x2, Pallas kernels, mix_rows(): pl.pallas_call(mix_kernel, grid=(groups, peers), in_specs=[pl.BlockSpec((...  60.1 us
    convert_element_type x2, other arithmetic, doc_backward(): dscore = (probs * (dprob - delta)).astype(jnp.bfloat16)  57.7 us
    dot_general x2, matrix products, doc_backward(): jnp.einsum('qhd,kd->hqk', grad_blk, value_blk, preferred_element_type=jnp...  50.8 us
  transfers between devices with their start and end apart: 13, of which 9 were waited for; matrix products, arithmetic and copies ran while one was open for 31% of the time, Pallas kernels for 11%

profile of v1, /device:TPU:0, one launch (start us, length us, event | category | flops | bytes accessed | tf_op | source)
XLA Modules:
  0.0 1142.7 jit_solution(4691244238917761331)
XLA Ops:
  6.5 1.0 constant_dynamic-slice_fusion.2
  7.5 2.4 pad_maximum_fusion.4
  10.0 0.7 all-gather.16.cloned.1.call-update
  10.8 5.4 copy.61
  16.2 3.1 copy.62
  19.3 2.4 constant_dynamic-slice_fusion.4
  21.7 242.6 %while.10 = (s32[]{:T(128)}, bf16[2,1024,1280]{2,1,0:T(8,128)(2,1)}, bf16[2,1024,128]{2,1,0:T(8,128)(2,1)}, bf16[2,1024,8,128]{3,2,1,0:T(8,128)(2,1)}, bf16[2,10...) while((s32[]{:T(128)}, bf16[2,1024,1280]{2,1,0:T(8,128)(2,1)}, ...), condition=%wide.region_6.7_spmd, body=%wide.region_2.6_spmd.sunk | while | flops 10857866240 | bytes 291964512 | solution.py:197
  21.9 4.1 constant_dynamic-slice_fusion.7
  26.0 0.3 iota_compare_fusion.3
  26.3 19.4 %fusion.96 = (f32[8,1024]{1,0:T(8,128)S(1)}, f32[8,1024,1024]{1,2,0:T(8,128)}) fusion(pred[1024,1024]{0,1:T(8,128)(4,1)S(1)} %iota_compare_fusion.3, bf16[1,1024,8,128]{3,2,1,0:T(8,128)(2,1)S(1)} %get-tuple-element.120, bf16[2,1024,128]{2,1,0:T(8,128)(2,1)} %get-tuple-element.141, s32[]{:T(128)} %get-tuple-element.132), kind=kOutput, calls=%fused_computation.95.clone.1 | convolution fusion | flops 2181039104 | bytes 36995584 | tf_op jit(solution)/shard_map/while/body/eval_jaxpr/sub | solution.py:106
  45.7 25.3 %fusion.98 = (f32[8,1024]{1,0:T(8,128)S(1)}, f32[1024,1024,8]{1,0,2:T(8,128)}) fusion(f32[8,1024,1024]{1,2,0:T(8,128)} %get-tuple-element.121, f32[8,1024]{1,0:T(8,128)S(1)} %get-tuple-element.122, bf16[1,1024,8,128]{3,2,1,0:T(8,128)(2,1)} %get-tuple-element.119, bf16[2,1024,128]{2,1,0:T(8,128)(2,1)} %get-tuple-element.143, s32[]{:T(128)} %get-tuple-element.132), kind=kOutput, calls=%fused_computation.3.clone.1 | convolution fusion | flops 2172641280 | bytes 69534208 | tf_op jit(solution)/shard_map/while/body/eval_jaxpr/qhd,kd->hqk/dot_general | solution.py:109
  71.0 29.7 %fusion.99 = bf16[8,1024,1024]{1,2,0:T(8,128)(2,1)} fusion(f32[1024,1024,8]{1,0,2:T(8,128)} %get-tuple-element.123, f32[8,1024]{1,0:T(8,128)S(1)} %get-tuple-element.124, f32[8,1024,1024]{1,2,0:T(8,128)} %get-tuple-element.121, f32[8,1024]{1,0:T(8,128)S(1)} %get-tuple-element.122), kind=kLoop, calls=%fused_computation.5.clone.1 | loop fusion | flops 33554432 | bytes 83951616 | tf_op jit(solution)/shard_map/while/body/eval_jaxpr/convert_element_type | solution.py:111
  100.8 9.8 multiply_convert_fusion.3
  110.6 11.5 %fusion.100 = bf16[1024,128]{0,1:T(8,128)(2,1)S(1)} fusion(bf16[8,1024,1024]{1,2,0:T(8,128)(2,1)} %fusion.99, bf16[1,1024,8,128]{3,2,1,0:T(8,128)(2,1)S(1)} %get-tuple-element.120), kind=kOutput, calls=%fused_computation.27.clone.1 | convolution fusion | flops 2147745792 | bytes 19136512 | tf_op jit(solution)/shard_map/while/body/eval_jaxpr/hqk,qhd->kd/dot_general | solution.py:116
  122.1 14.3 %fusion.97 = bf16[1024,128]{0,1:T(8,128)(2,1)S(1)} fusion(bf16[1,1024,8,128]{3,2,1,0:T(8,128)(2,1)} %get-tuple-element.119, f32[8,1024,1024]{1,2,0:T(8,128)} %get-tuple-element.121, f32[8,1024]{1,0:T(8,128)S(1)} %get-tuple-element.122), kind=kOutput, calls=%fused_computation.28.clone.1 | convolution fusion | flops 2164391936 | bytes 35946496 | tf_op jit(solution)/shard_map/while/body/eval_jaxpr/hqk,qhd->kd/dot_general | solution.py:118
  136.4 1.9 maximum_bitcast_fusion.2
  138.2 2.7 copy.99
  140.9 3.4 constant_dynamic-update-slice_fusion.2
  144.3 3.8 constant_dynamic-slice_fusion.7
  148.1 0.3 iota_compare_fusion.3
  148.5 18.8 %fusion.96 = (f32[8,1024]{1,0:T(8,128)S(1)}, f32[8,1024,1024]{1,2,0:T(8,128)}) fusion(pred[1024,1024]{0,1:T(8,128)(4,1)S(1)} %iota_compare_fusion.3, bf16[1,1024,8,128]{3,2,1,0:T(8,128)(2,1)S(1)} %get-tuple-element.120, bf16[2,1024,128]{2,1,0:T(8,128)(2,1)} %get-tuple-element.141, s32[]{:T(128)} %get-tuple-element.132), kind=kOutput, calls=%fused_computation.95.clone.1 | convolution fusion | flops 2181039104 | bytes 36995584 | tf_op jit(solution)/shard_map/while/body/eval_jaxpr/sub | solution.py:106
  167.3 25.5 %fusion.98 = (f32[8,1024]{1,0:T(8,128)S(1)}, f32[1024,1024,8]{1,0,2:T(8,128)}) fusion(f32[8,1024,1024]{1,2,0:T(8,128)} %get-tuple-element.121, f32[8,1024]{1,0:T(8,128)S(1)} %get-tuple-element.122, bf16[1,1024,8,128]{3,2,1,0:T(8,128)(2,1)} %get-tuple-element.119, bf16[2,1024,128]{2,1,0:T(8,128)(2,1)} %get-tuple-element.143, s32[]{:T(128)} %get-tuple-element.132), kind=kOutput, calls=%fused_computation.3.clone.1 | convolution fusion | flops 2172641280 | bytes 69534208 | tf_op jit(solution)/shard_map/while/body/eval_jaxpr/qhd,kd->hqk/dot_general | solution.py:109
  192.7 28.0 %fusion.99 = bf16[8,1024,1024]{1,2,0:T(8,128)(2,1)} fusion(f32[1024,1024,8]{1,0,2:T(8,128)} %get-tuple-element.123, f32[8,1024]{1,0:T(8,128)S(1)} %get-tuple-element.124, f32[8,1024,1024]{1,2,0:T(8,128)} %get-tuple-element.121, f32[8,1024]{1,0:T(8,128)S(1)} %get-tuple-element.122), kind=kLoop, calls=%fused_computation.5.clone.1 | loop fusion | flops 33554432 | bytes 83951616 | tf_op jit(solution)/shard_map/while/body/eval_jaxpr/convert_element_type | solution.py:111
  220.7 9.7 multiply_convert_fusion.3
  230.4 11.4 %fusion.100 = bf16[1024,128]{0,1:T(8,128)(2,1)S(1)} fusion(bf16[8,1024,1024]{1,2,0:T(8,128)(2,1)} %fusion.99, bf16[1,1024,8,128]{3,2,1,0:T(8,128)(2,1)S(1)} %get-tuple-element.120), kind=kOutput, calls=%fused_computation.27.clone.1 | convolution fusion | flops 2147745792 | bytes 19136512 | tf_op jit(solution)/shard_map/while/body/eval_jaxpr/hqk,qhd->kd/dot_general | solution.py:116
  241.9 14.1 %fusion.97 = bf16[1024,128]{0,1:T(8,128)(2,1)S(1)} fusion(bf16[1,1024,8,128]{3,2,1,0:T(8,128)(2,1)} %get-tuple-element.119, f32[8,1024,1024]{1,2,0:T(8,128)} %get-tuple-element.121, f32[8,1024]{1,0:T(8,128)S(1)} %get-tuple-element.122), kind=kOutput, calls=%fused_computation.28.clone.1 | convolution fusion | flops 2164391936 | bytes 35946496 | tf_op jit(solution)/shard_map/while/body/eval_jaxpr/hqk,qhd->kd/dot_general | solution.py:118
  256.0 1.8 maximum_bitcast_fusion.2
  257.8 2.7 copy.99
  260.5 3.4 constant_dynamic-update-slice_fusion.2
  264.3 10.2 convolution_convert_fusion.3
  274.5 15.5 %all-gather = s32[2048,8]{0,1:T(8,128)S(1)} all-gather(s32[512,8]{0,1:T(8,128)S(1)} %copy-done.5), channel_id=2, replica_groups=mesh['section'=2,'row'=4,'col'=4] {'row'}, dimensions={0}, use_global_device_ids=true | all-gather | bytes 81920 | tf_op jit(solution)/shard_map/all_gather | solution.py:160
  290.0 0.6 copy-done.3
  291.1 0.7 broadcast_in_dim.53.pos_ref
  291.8 27.1 %pick_rows.5 = bf16[8,4,144,2048]{3,2,1,0:T(8,128)(2,1)} custom-call(s32[8,4,1,512]{3,2,1,0:T(1,128)} %broadcast_in_dim.53.pos_ref, bf16[4,512,2048]{2,1,0:T(8,128)(2,1)} %bitcast.170), custom_call_target="tpu_custom_call" | custom-call | flops 9663676416 | bytes 27262976 | tf_op jit(solution)/shard_map/pick_rows/pallas_call | solution.py:31
  318.8 6.0 all-to-all-start.2
  324.8 10.3 convolution_convert_fusion.2
  335.2 18.9 %reduce-scatter.5.cloned.1.call-done = bf16[512,1024]{1,0:T(8,128)(2,1)} async-done(((bf16[2048,1024]{1,0:T(8,128)(2,1)}), bf16[512,1024]{1,0:T(8,128)(2,1)}) %reduce-scatter.5.cloned.1.call-update) | async-done | bytes 1048592 | tf_op jit(solution)/shard_map/reduce_scatter | solution.py:213
  354.1 79.3 %reduce-scatter.7.cloned.1.call-done = bf16[512,1024]{1,0:T(8,128)(2,1)} async-done(((bf16[2048,1024]{1,0:T(8,128)(2,1)}), bf16[512,1024]{1,0:T(8,128)(2,1)}) %reduce-scatter.7.cloned.1.call-update) | async-done | bytes 1048592 | tf_op jit(solution)/shard_map/reduce_scatter | solution.py:213
  433.4 3.8 add_convert_fusion
  437.3 81.4 %all-gather.12.cloned.1.call-done = bf16[2048,1024]{1,0:T(8,128)(2,1)} async-done(((bf16[512,1024]{1,0:T(8,128)(2,1)}), bf16[2048,1024]{1,0:T(8,128)(2,1)}) %all-gather.12.cloned.1.call-update) | async-done | bytes 4194320 | tf_op jit(solution)/shard_map/all_gather | solution.py:218
  518.7 21.6 %pick_rows.3 = bf16[8,4,144,1024]{3,2,1,0:T(8,128)(2,1)} custom-call(s32[8,4,1,512]{3,2,1,0:T(1,128)} %broadcast_in_dim.53.pos_ref, bf16[4,512,1024]{2,1,0:T(8,128)(2,1)} %bitcast.173), custom_call_target="tpu_custom_call" | custom-call | flops 4831838208 | bytes 13631488 | tf_op jit(solution)/shard_map/pick_rows/pallas_call | solution.py:31
  540.3 5.0 all-to-all-start
  545.4 0.5 all-gather.14.cloned.1.call-update
  545.9 81.2 %all-gather.14.cloned.1.call-done = bf16[2048,1024]{1,0:T(8,128)(2,1)} async-done(((bf16[512,1024]{1,0:T(8,128)(2,1)}), bf16[2048,1024]{1,0:T(8,128)(2,1)}) %all-gather.14.cloned.1.call-update) | async-done | bytes 4194320 | tf_op jit(solution)/shard_map/all_gather | solution.py:218
  627.1 21.5 %pick_rows.4 = bf16[8,4,144,1024]{3,2,1,0:T(8,128)(2,1)} custom-call(s32[8,4,1,512]{3,2,1,0:T(1,128)} %broadcast_in_dim.53.pos_ref, bf16[4,512,1024]{2,1,0:T(8,128)(2,1)} %bitcast.174), custom_call_target="tpu_custom_call" | custom-call | flops 4831838208 | bytes 13631488 | tf_op jit(solution)/shard_map/pick_rows/pallas_call | solution.py:31
  648.5 1.5 all-to-all-done
  650.0 5.2 all-to-all-start.1
  655.2 36.8 %fusion.47 = f32[4608,1536]{0,1:T(8,128)} fusion(bf16[4608,2048]{1,0:T(8,128)(2,1)} %bitcast.26, bf16[1,2048,1536]{2,1,0:T(8,128)(2,1)} %param.26), kind=kOutput, calls=%fused_computation.56 | convolution fusion | flops 28991029248 | bytes 53477376 | tf_op jit(solution)/shard_map/dot_general | solution.py:190
  692.0 13.8 %fusion.56 = f32[4608,768]{0,1:T(8,128)} fusion(bf16[4608,1024]{1,0:T(8,128)(2,1)} %bitcast.21, bf16[768,2048]{1,0:T(8,128)(2,1)S(1)} %bitcast.175), kind=kOutput, calls=%fused_computation.70 | convolution fusion | flops 7247757312 | bytes 25165824 | tf_op jit(solution)/shard_map/dot_general | solution.py:220
  705.8 54.1 %all-to-all-done.1 = bf16[8,4,144,1024]{3,2,1,0:T(8,128)(2,1)} async-done(((bf16[8,4,144,1024]{3,2,1,0:T(8,128)(2,1)}), bf16[8,4,144,1024]{3,2,1,0:T(8,128)(2,1)}, u32[]{:S(2)}, u32[]{:S(2)}) %all-to-all-start.1) | async-done | bytes 9437216 | tf_op jit(solution)/shard_map/all_to_all | solution.py:182
  759.9 28.1 %fusion.46 = (bf16[4608,768]{0,1:T(8,128)(2,1)}, bf16[4608,768]{0,1:T(8,128)(2,1)}) fusion(f32[4608,1536]{0,1:T(8,128)} %fusion.47, f32[4608,768]{0,1:T(8,128)} %fusion.56, bf16[4608,1024]{1,0:T(8,128)(2,1)} %bitcast.24, bf16[768,2048]{1,0:T(8,128)(2,1)S(1)} %bitcast.176), kind=kOutput, calls=%fused_computation.49 | convolution fusion | flops 7297302528 | bytes 67633152 | tf_op jit(solution)/shard_map/dot_general | solution.py:220
  788.0 20.7 %convolution_convert_fusion.1 = bf16[4608,1024]{1,0:T(8,128)(2,1)} fusion(bf16[4608,768]{0,1:T(8,128)(2,1)} %get-tuple-element.69, bf16[4608,768]{0,1:T(8,128)(2,1)} %get-tuple-element.68, bf16[1,2048,1536]{2,1,0:T(8,128)(2,1)} %param.26), kind=kOutput, calls=%fused_computation.54 | convolution fusion | flops 14528544768 | bytes 26738688 | tf_op jit(solution)/shard_map/dot_general | solution.py:238
  808.7 5.2 all-to-all-start.3
  813.9 13.2 %all-gather.1 = f32[2048,8]{0,1:T(8,128)S(1)} all-gather(f32[512,8]{0,1:T(8,128)S(1)} %copy-done.6), channel_id=3, replica_groups=mesh['section'=2,'row'=4,'col'=4] {'row'}, dimensions={0}, use_global_device_ids=true | all-gather | bytes 81920 | tf_op jit(solution)/shard_map/all_gather | solution.py:161
  827.1 0.2 fusion.61
  827.3 0.7 broadcast_in_dim.56.weight_ref
  828.0 20.4 %convolution_convert_fusion = bf16[4608,1024]{1,0:T(8,128)(2,1)} fusion(bf16[4608,768]{0,1:T(8,128)(2,1)} %get-tuple-element.69, bf16[4608,768]{0,1:T(8,128)(2,1)} %get-tuple-element.68, bf16[1,2048,1536]{2,1,0:T(8,128)(2,1)} %param.26), kind=kOutput, calls=%fused_computation.53 | convolution fusion | flops 14528544768 | bytes 26738688 | tf_op jit(solution)/shard_map/dot_general | solution.py:238
  848.4 70.1 %all-to-all-done.3.rows_ref = bf16[8,4,144,1024]{3,2,1,0:T(8,128)(2,1)} async-done(((bf16[8,4,144,1024]{3,2,1,0:T(8,128)(2,1)}), bf16[8,4,144,1024]{3,2,1,0:T(8,128)(2,1)}, u32[]{:S(2)}, u32[]{:S(2)}) %all-to-all-start.3) | async-done | bytes 9437216 | tf_op jit(solution)/shard_map/all_to_all | solution.py:182
  918.6 5.1 all-to-all-start.4
  923.7 30.1 %mix_rows.2 = bf16[2048,1024]{1,0:T(8,128)(2,1)} custom-call(s32[8,4,1,512]{3,2,1,0:T(1,128)} %broadcast_in_dim.53.pos_ref, f32[8,4,1,512]{3,2,1,0:T(1,128)} %broadcast_in_dim.56.weight_ref, bf16[8,4,144,1024]{3,2,1,0:T(8,128)(2,1)} %all-to-all-done.3.rows_ref), custom_call_target="tpu_custom_call" | custom-call | flops 4831838208 | bytes 13631488 | tf_op jit(solution)/shard_map/mix_rows/pallas_call | solution.py:75
  953.9 74.4 %all-to-all-done.4.rows_ref = bf16[8,4,144,1024]{3,2,1,0:T(8,128)(2,1)} async-done(((bf16[8,4,144,1024]{3,2,1,0:T(8,128)(2,1)}), bf16[8,4,144,1024]{3,2,1,0:T(8,128)(2,1)}, u32[]{:S(2)}, u32[]{:S(2)}) %all-to-all-start.4) | async-done | bytes 9437216 | tf_op jit(solution)/shard_map/all_to_all | solution.py:182
  1028.3 30.0 %mix_rows.3 = bf16[2048,1024]{1,0:T(8,128)(2,1)} custom-call(s32[8,4,1,512]{3,2,1,0:T(1,128)} %broadcast_in_dim.53.pos_ref, f32[8,4,1,512]{3,2,1,0:T(1,128)} %broadcast_in_dim.56.weight_ref, bf16[8,4,144,1024]{3,2,1,0:T(8,128)(2,1)} %all-to-all-done.4.rows_ref), custom_call_target="tpu_custom_call" | custom-call | flops 4831838208 | bytes 13631488 | tf_op jit(solution)/shard_map/mix_rows/pallas_call | solution.py:75
  1058.4 74.2 %reduce-scatter.11.cloned.1.call-done = bf16[512,1024]{1,0:T(8,128)(2,1)} async-done(((bf16[2048,1024]{1,0:T(8,128)(2,1)}), bf16[512,1024]{1,0:T(8,128)(2,1)}) %reduce-scatter.11.cloned.1.call-update) | async-done | bytes 1048592 | tf_op jit(solution)/shard_map/reduce_scatter | solution.py:246
  1132.6 3.1 pad_maximum_fusion.3
  (43 shorter events, 0.9 us)
Async XLA Ops:
  6.5 257.8 %all-gather.10.cloned.1.call-start = ((), (), s32[]{:S(2)}) async-start(), calls=%async_computation.9 | async-start | bytes 6553600 | tf_op jit(solution)/shard_map/all_gather | solution.py:150
  9.9 281.8 %all-gather.16.cloned.1.call-start = ((), (), s32[]{:S(2)}) async-start(), calls=%async_computation.16 | async-start | bytes 10485760 | tf_op jit(solution)/shard_map/all_gather | solution.py:162
  10.7 343.4 %reduce-scatter.5.cloned.1.call-start = ((), (), s32[]{:S(2)}) async-start(), calls=%async_computation.10 | async-start | bytes 5242880 | tf_op jit(solution)/shard_map/reduce_scatter | solution.py:213
  10.8 5.4 copy-start.1
  71.0 29.7 %copy-start = (bf16[2,1024,128]{2,1,0:T(8,128)(2,1)S(1)}, bf16[2,1024,128]{2,1,0:T(8,128)(2,1)}, u32[]{:S(2)}) copy-start(bf16[2,1024,128]{2,1,0:T(8,128)(2,1)} %get-tuple-element.141) | copy-start | bytes 1572868 | tf_op jit(solution)/shard_map/while
  192.7 28.0 %copy-start = (bf16[2,1024,128]{2,1,0:T(8,128)(2,1)S(1)}, bf16[2,1024,128]{2,1,0:T(8,128)(2,1)}, u32[]{:S(2)}) copy-start(bf16[2,1024,128]{2,1,0:T(8,128)(2,1)} %get-tuple-element.141) | copy-start | bytes 1572868 | tf_op jit(solution)/shard_map/while
  264.3 10.2 copy-start.5
  290.0 0.6 copy-start.3
  290.0 1.1 copy-start.7
  318.8 221.5 %all-to-all-start.2 = ((bf16[8,4,144,2048]{3,2,1,0:T(8,128)(2,1)}), bf16[8,4,144,2048]{3,2,1,0:T(8,128)(2,1)}, u32[]{:S(2)}, u32[]{:S(2)}) async-start(bf16[8,4,144,2048]{3,2,1,0:T(8,128)(2,1)} %pick_rows.5), calls=%async_computation.4 | async-start | bytes 37748736 | tf_op jit(solution)/shard_map/all_to_all | solution.py:182
  324.8 108.6 %copy-start.2 = (bf16[512,2048]{1,0:T(8,128)(2,1)S(1)}, bf16[512,2048]{1,0:T(8,128)(2,1)}, u32[]{:S(2)}) copy-start(bf16[512,2048]{1,0:T(8,128)(2,1)} %param.22) | copy-start | bytes 6291460
  324.8 108.6 %reduce-scatter.7.cloned.1.call-start = ((), (), s32[]{:S(2)}) async-start(), calls=%async_computation.11 | async-start | bytes 5242880 | tf_op jit(solution)/shard_map/reduce_scatter | solution.py:213
  335.2 183.5 %all-gather.12.cloned.1.call-start = ((), (), s32[]{:S(2)}) async-start(), calls=%async_computation.14 | async-start | bytes 5242880 | tf_op jit(solution)/shard_map/all_gather | solution.py:218
  540.3 109.7 %all-to-all-start = ((bf16[8,4,144,1024]{3,2,1,0:T(8,128)(2,1)}), bf16[8,4,144,1024]{3,2,1,0:T(8,128)(2,1)}, u32[]{:S(2)}, u32[]{:S(2)}) async-start(bf16[8,4,144,1024]{3,2,1,0:T(8,128)(2,1)} %pick_rows.3), calls=%async_computation.1 | async-start | bytes 18874368 | tf_op jit(solution)/shard_map/all_to_all | solution.py:182
  545.3 81.7 %all-gather.14.cloned.1.call-start = ((), (), s32[]{:S(2)}) async-start(), calls=%async_computation.15 | async-start | bytes 5242880 | tf_op jit(solution)/shard_map/all_gather | solution.py:218
  650.0 109.9 %all-to-all-start.1 = ((bf16[8,4,144,1024]{3,2,1,0:T(8,128)(2,1)}), bf16[8,4,144,1024]{3,2,1,0:T(8,128)(2,1)}, u32[]{:S(2)}, u32[]{:S(2)}) async-start(bf16[8,4,144,1024]{3,2,1,0:T(8,128)(2,1)} %pick_rows.4), calls=%async_computation.3 | async-start | bytes 18874368 | tf_op jit(solution)/shard_map/all_to_all | solution.py:182
  655.2 36.8 %copy-start.9 = (bf16[1,768,2048]{2,1,0:T(8,128)(2,1)S(1)}, bf16[1,768,2048]{2,1,0:T(8,128)(2,1)}, u32[]{:S(2)}) copy-start(bf16[1,768,2048]{2,1,0:T(8,128)(2,1)} %param.27) | copy-start | bytes 9437188
  808.7 5.2 copy-start.6
  808.7 18.4 %copy-start.4 = (s32[2048,8]{0,1:T(8,128)S(1)}, s32[2048,8]{0,1:T(8,128)}, u32[]{:S(2)}) copy-start(s32[2048,8]{0,1:T(8,128)} %copy-done.3) | copy-start | bytes 196612
  808.7 18.4 %copy-start.8 = (s32[8]{0:T(128)S(1)}, s32[8]{0:T(128)}, u32[]{:S(2)}) copy-start(s32[8]{0:T(128)} %copy-done.7) | copy-start | bytes 100
  808.7 109.9 %all-to-all-start.3 = ((bf16[8,4,144,1024]{3,2,1,0:T(8,128)(2,1)}), bf16[8,4,144,1024]{3,2,1,0:T(8,128)(2,1)}, u32[]{:S(2)}, u32[]{:S(2)}) async-start(bf16[8,4,144,1024]{3,2,1,0:T(8,128)(2,1)} %bitcast.162), calls=%async_computation.5 | async-start | bytes 18874368 | tf_op jit(solution)/shard_map/all_to_all | solution.py:182
  918.6 109.7 %all-to-all-start.4 = ((bf16[8,4,144,1024]{3,2,1,0:T(8,128)(2,1)}), bf16[8,4,144,1024]{3,2,1,0:T(8,128)(2,1)}, u32[]{:S(2)}, u32[]{:S(2)}) async-start(bf16[8,4,144,1024]{3,2,1,0:T(8,128)(2,1)} %bitcast.161), calls=%async_computation.7 | async-start | bytes 18874368 | tf_op jit(solution)/shard_map/all_to_all | solution.py:182
  923.6 134.8 %reduce-scatter.9.cloned.1.call-start = ((), (), s32[]{:S(2)}) async-start(), calls=%async_computation.12 | async-start | bytes 5242880 | tf_op jit(solution)/shard_map/reduce_scatter | solution.py:246
  953.8 178.8 %reduce-scatter.11.cloned.1.call-start = ((), (), s32[]{:S(2)}) async-start(), calls=%async_computation.13 | async-start | bytes 5242880 | tf_op jit(solution)/shard_map/reduce_scatter | solution.py:246
Sparse Core Ops, SparseCore 0:
  10.1 64.0 all-gather.9
  75.7 149.5 all-gather.15
  274.6 79.4 reduce-scatter.4
  356.2 77.1 reduce-scatter.6
  437.4 81.2 all-gather.11
  547.4 79.6 all-gather.13
  954.0 75.6 reduce-scatter.8
  1058.5 74.0 reduce-scatter.10

commit v2 on v1

--- a/solution.py
+++ b/solution.py
@@ -1,5 +1,3 @@
-from functools import partial
-
 import jax
 import jax.numpy as jnp
 from jax import lax
@@ -12,30 +10,46 @@
 HEAD_DIM = 128
 TOPK = 8
 DOC = 1024
-CHUNKS = 2
+CHUNKS = 4
+PART = 512
+ATT_BLOCK = 256
+LOG2_E = 1.4426950408889634
+
+
+def slot_hits(pos, cap):
+    slot = lax.broadcasted_iota(jnp.int32, (cap, pos.shape[1]), 0)
+    return slot == pos
 
 
 def pick_kernel(pos_ref, rows_ref, out_ref):
-    cap = out_ref.shape[2]
-    tokens = rows_ref.shape[1]
-    pos = pos_ref[0, 0]
-    slot = lax.broadcasted_iota(jnp.int32, (cap, tokens), 0)
-    onehot = jnp.where(slot == pos, 1.0, 0.0).astype(jnp.bfloat16)
-    picked = jnp.dot(onehot, rows_ref[0], preferred_element_type=jnp.float32)
-    out_ref[0, 0] = picked.astype(out_ref.dtype)
+    peers, _, cap, width = out_ref.shape
+    picks = [
+        jnp.where(slot_hits(pos_ref[p, 0], cap), 1.0, 0.0).astype(jnp.bfloat16)
+        for p in range(peers)
+    ]
+    if cap % 16 == 0:
+        picked = jnp.dot(
+            jnp.concatenate(picks, axis=0), rows_ref[0], preferred_element_type=jnp.float32
+        ).astype(out_ref.dtype)
+        out_ref[:, 0] = picked.reshape(peers, cap, width)
+    else:
+        for p in range(peers):
+            picked = jnp.dot(picks[p], rows_ref[0], preferred_element_type=jnp.float32)
+            out_ref[p, 0] = picked.astype(out_ref.dtype)
 
 
 def pick_rows(pos, rows, cap):
     peers, groups, _, tokens = pos.shape
     width = rows.shape[2]
+    part = min(PART, width)
     return pl.pallas_call(
         pick_kernel,
-        grid=(groups, peers),
+        grid=(groups, width // part),
         in_specs=[
-            pl.BlockSpec((1, 1, 1, tokens), lambda g, p: (p, g, 0, 0)),
-            pl.BlockSpec((1, tokens, width), lambda g, p: (g, 0, 0)),
+            pl.BlockSpec((peers, 1, 1, tokens), lambda g, w: (0, g, 0, 0)),
+            pl.BlockSpec((1, tokens, part), lambda g, w: (g, 0, w)),
         ],
-        out_specs=pl.BlockSpec((1, 1, cap, width), lambda g, p: (p, g, 0, 0)),
+        out_specs=pl.BlockSpec((peers, 1, cap, part), lambda g, w: (0, g, 0, w)),
         out_shape=jax.ShapeDtypeStruct((peers, groups, cap, width), rows.dtype),
         cost_estimate=pl.CostEstimate(
             flops=2 * peers * groups * cap * tokens * width,
@@ -46,43 +60,43 @@
     )(pos, rows)
 
 
-def mix_kernel(pos_ref, weight_ref, rows_ref, out_ref, total_ref):
-    peer = pl.program_id(1)
-    cap = rows_ref.shape[2]
-    tokens = out_ref.shape[0]
-    slot = lax.broadcasted_iota(jnp.int32, (cap, tokens), 0)
-    spread = jnp.where(slot == pos_ref[0, 0], weight_ref[0, 0], 0.0).astype(jnp.bfloat16)
-    term = lax.dot_general(
-        spread, rows_ref[0, 0], (((0,), (0,)), ((), ())), preferred_element_type=jnp.float32
-    )
-
-    @pl.when(peer == 0)
-    def _():
-        total_ref[...] = term
-
-    @pl.when(peer > 0)
-    def _():
-        total_ref[...] += term
-
-    @pl.when(peer == pl.num_programs(1) - 1)
-    def _():
-        out_ref[...] = total_ref[...].astype(out_ref.dtype)
+def mix_kernel(pos_ref, weight_ref, rows_ref, out_ref):
+    peers, _, cap, width = rows_ref.shape
+    spreads = [
+        jnp.where(slot_hits(pos_ref[p, 0], cap), weight_ref[p, 0], 0.0).astype(jnp.bfloat16)
+        for p in range(peers)
+    ]
+    across = (((0,), (0,)), ((), ()))
+    if cap % 16 == 0:
+        total = lax.dot_general(
+            jnp.concatenate(spreads, axis=0),
+            rows_ref[:, 0].reshape(peers * cap, width),
+            across,
+            preferred_element_type=jnp.float32,
+        )
+    else:
+        total = jnp.zeros(out_ref.shape, jnp.float32)
+        for p in range(peers):
+            total += lax.dot_general(
+                spreads[p], rows_ref[p, 0], across, preferred_element_type=jnp.float32
+            )
+    out_ref[...] = total.astype(out_ref.dtype)
 
 
 def mix_rows(pos, weight, rows):
     peers, groups, _, tokens = pos.shape
     cap, width = rows.shape[2:]
+    part = min(PART, width)
     return pl.pallas_call(
         mix_kernel,
-        grid=(groups, peers),
+        grid=(groups, width // part),
         in_specs=[
-            pl.BlockSpec((1, 1, 1, tokens), lambda g, p: (p, g, 0, 0)),
-            pl.BlockSpec((1, 1, 1, tokens), lambda g, p: (p, g, 0, 0)),
-            pl.BlockSpec((1, 1, cap, width), lambda g, p: (p, g, 0, 0)),
+            pl.BlockSpec((peers, 1, 1, tokens), lambda g, w: (0, g, 0, 0)),
+            pl.BlockSpec((peers, 1, 1, tokens), lambda g, w: (0, g, 0, 0)),
+            pl.BlockSpec((peers, 1, cap, part), lambda g, w: (0, g, 0, w)),
         ],
-        out_specs=pl.BlockSpec((tokens, width), lambda g, p: (g, 0)),
+        out_specs=pl.BlockSpec((tokens, part), lambda g, w: (g, w)),
         out_shape=jax.ShapeDtypeStruct((groups * tokens, width), rows.dtype),
-        scratch_shapes=[pltpu.VMEM((tokens, width), jnp.float32)],
         cost_estimate=pl.CostEstimate(
             flops=2 * peers * groups * cap * tokens * width,
             bytes_accessed=2 * width * groups * (tokens + peers * cap),
@@ -92,35 +106,83 @@
     )(pos, weight, rows)
 
 
-def doc_backward(block, scale_val):
-    query_blk, grad_blk, key_blk, value_blk = block
-    doc_len = query_blk.shape[0]
-    heads_here = query_blk.shape[1]
-    causal = jnp.arange(doc_len)[:, None] >= jnp.arange(doc_len)[None, :]
-    scores = (
-        jnp.einsum("qhd,kd->hqk", query_blk, key_blk, preferred_element_type=jnp.float32)
-        * scale_val
-    )
-    scores = jnp.where(causal[None], scores, -jnp.inf)
-    top = jnp.max(scores, axis=-1, keepdims=True)
-    expo = jnp.exp(scores - top)
-    probs = expo / jnp.sum(expo, axis=-1, keepdims=True)
-    probs_b = probs.astype(jnp.bfloat16)
-    dprob = jnp.einsum("qhd,kd->hqk", grad_blk, value_blk, preferred_element_type=jnp.float32)
-    delta = jnp.sum(probs * dprob, axis=-1, keepdims=True)
-    dscore = (probs * (dprob - delta)).astype(jnp.bfloat16)
-    dquery = (
-        jnp.einsum("hqk,kd->qhd", dscore, key_blk, preferred_element_type=jnp.float32) * scale_val
-    ).astype(jnp.bfloat16)
-    dkey = (
-        jnp.einsum("hqk,qhd->kd", dscore, query_blk, preferred_element_type=jnp.float32) * scale_val
-    ).astype(jnp.bfloat16)
-    dvalue = jnp.einsum(
-        "hqk,qhd->kd", probs_b, grad_blk, preferred_element_type=jnp.float32
-    ).astype(jnp.bfloat16)
-    return jnp.concatenate(
-        [dquery.reshape(doc_len, heads_here * key_blk.shape[1]), dkey, dvalue], axis=1
-    )
+def doc_kernel(query_ref, grad_ref, key_ref, value_ref, out_ref, dkey_ref, dvalue_ref):
+    head = pl.program_id(1)
+    doc_len, dim = query_ref.shape
+    scale_val = dim ** (-0.5)
+    block = min(ATT_BLOCK, doc_len)
+
+    @pl.when(head == 0)
+    def _():
+        dkey_ref[...] = jnp.zeros_like(dkey_ref)
+        dvalue_ref[...] = jnp.zeros_like(dvalue_ref)
+
+    key_turned = key_ref[...].T
+    columns = pl.ds(pl.multiple_of(head * dim, dim), dim)
+    for at in range(0, doc_len, block):
+        seen = at + block
+        query = query_ref[at:seen, :]
+        grad = grad_ref[at:seen, :]
+        scores = lax.dot_general(
+            key_ref[:seen, :],
+            query,
+            (((1,), (1,)), ((), ())),
+            preferred_element_type=jnp.float32,
+        )
+        key_at = lax.broadcasted_iota(jnp.int32, (block, block), 0)
+        query_at = lax.broadcasted_iota(jnp.int32, (block, block), 1)
+        corner = jnp.where(key_at <= query_at, scores[at:, :], -jnp.inf)
+        scores = jnp.concatenate([scores[:at, :], corner], axis=0) if at else corner
+        top = jnp.max(scores, axis=0, keepdims=True)
+        expo = jnp.exp2((scores - top) * (scale_val * LOG2_E))
+        probs = expo * (1.0 / jnp.sum(expo, axis=0, keepdims=True))
+        dprob = lax.dot_general(
+            value_ref[:seen, :],
+            grad,
+            (((1,), (1,)), ((), ())),
+            preferred_element_type=jnp.float32,
+        )
+        delta = jnp.sum(probs * dprob, axis=0, keepdims=True)
+        dscore = (probs * (dprob - delta)).astype(jnp.bfloat16)
+        dvalue_ref[:seen, :] += jnp.dot(
+            probs.astype(jnp.bfloat16), grad, preferred_element_type=jnp.float32
+        )
+        dkey_ref[:seen, :] += jnp.dot(dscore, query, preferred_element_type=jnp.float32)
+        turned = jnp.dot(key_turned[:, :seen], dscore, preferred_element_type=jnp.float32)
+        out_ref[at:seen, columns] = (turned.T * scale_val).astype(out_ref.dtype)
+
+    @pl.when(head == pl.num_programs(1) - 1)
+    def _():
+        heads = out_ref.shape[1] // dim - 2
+        out_ref[:, heads * dim : (heads + 1) * dim] = (dkey_ref[...] * scale_val).astype(
+            out_ref.dtype
+        )
+        out_ref[:, (heads + 1) * dim :] = dvalue_ref[...].astype(out_ref.dtype)
+
+
+def attention_backward(queries, out_grad, key_head, value_head):
+    rows, width = queries.shape
+    dim = key_head.shape[1]
+    docs, heads = rows // DOC, width // dim
+    return pl.pallas_call(
+        doc_kernel,
+        grid=(docs, heads),
+        in_specs=[
+            pl.BlockSpec((DOC, dim), lambda d, h: (d, h)),
+            pl.BlockSpec((DOC, dim), lambda d, h: (d, h)),
+            pl.BlockSpec((DOC, dim), lambda d, h: (d, 0)),
+            pl.BlockSpec((DOC, dim), lambda d, h: (d, 0)),
+        ],
+        out_specs=pl.BlockSpec((DOC, width + 2 * dim), lambda d, h: (d, 0)),
+        out_shape=jax.ShapeDtypeStruct((rows, width + 2 * dim), queries.dtype),
+        scratch_shapes=[pltpu.VMEM((DOC, dim), jnp.float32)] * 2,
+        cost_estimate=pl.CostEstimate(
+            flops=10 * docs * heads * DOC * DOC * dim,
+            bytes_accessed=2 * rows * (3 * width + 4 * dim),
+            transcendentals=docs * heads * DOC * DOC,
+        ),
+        name="doc_backward",
+    )(queries, out_grad, key_head, value_head)
 
 
 def body(
@@ -157,9 +219,18 @@
     model = q_weight.shape[0] * col_count
     capacity = max(2, 9 * moe_rows * TOPK // (8 * n_experts))
 
-    ids_line = lax.all_gather(expert_ids, "row", axis=0, tiled=False)
-    weights_line = lax.all_gather(route_weights, "row", axis=0, tiled=False)
-    rows_line = lax.all_gather(moe_input, "row", axis=0, tiled=False)
+    routes = jnp.concatenate([expert_ids.astype(jnp.float32), route_weights], axis=1)
+    routes_line = lax.all_gather(routes, "row", axis=0, tiled=False)
+    routes_line, moe_input = lax.optimization_barrier((routes_line, moe_input))
+    ids_line = routes_line[..., :TOPK].astype(jnp.int32)
+    weights_line = routes_line[..., TOPK:]
+    rows_line = lax.all_to_all(
+        jnp.broadcast_to(moe_input[None], (row_count,) + moe_input.shape),
+        "row",
+        split_axis=0,
+        concat_axis=0,
+        tiled=True,
+    )
     peer = jnp.arange(peers, dtype=jnp.int32)
     peer_expert = (
         (peer // col_count) * row_count + lax.axis_index("row")
@@ -189,16 +260,7 @@
     rows_in = swap(pick_rows(pos, rows_line, capacity)).reshape(-1, model)
     gate_up = jnp.dot(rows_in, w_gu, preferred_element_type=jnp.float32)
 
-    doc_count = tok_rows // DOC
-    query_docs = queries.reshape(doc_count, DOC, heads_here, HEAD_DIM)
-    grad_docs = out_grad.reshape(doc_count, DOC, heads_here, HEAD_DIM)
-    key_docs = key_head.reshape(doc_count, DOC, HEAD_DIM)
-    value_docs = value_head.reshape(doc_count, DOC, HEAD_DIM)
-    dqkv = lax.map(
-        partial(doc_backward, scale_val=HEAD_DIM ** (-0.5)),
-        (query_docs, grad_docs, key_docs, value_docs),
-    )
-    dqkv = dqkv.reshape(tok_rows, dqkv.shape[-1])
+    dqkv = attention_backward(queries, out_grad, key_head, value_head)
 
     span = model // CHUNKS
     dhidden = None

time: 1150 us -> 1280 us (1.11)
  waiting for transfers between devices: 536 us -> 861 us
  matrix products: 300 us -> 176 us
  other arithmetic: 71.8 us -> 9.96 us
  starting transfers between devices: 26.8 us -> 58.3 us
  local copies, waits for them, and re-layouts: 34.1 us -> 9.76 us
  blocking collectives: 28.7 us -> 15.2 us
    reduce_scatter x2 -> x4, waiting for transfers between devices: 98.2 us -> 290 us  [body(): lax.psum_scatter(term.astype(jnp.bfloat16), 'row', scatter_dimension=0, t...]
    all_to_all x5 -> x9, waiting for transfers between devices: 200 us -> 335 us  [swap(): lax.all_to_all(blocks, ('section', 'col'), split_axis=0, concat_axis=0, t...]
    dot_general x8 -> x0, matrix products: 122 us -> none  [the longest x2 50.8 us: doc_backward(): jnp.einsum('qhd,kd->hqk', grad_blk, value_blk, preferred_element_type=jnp...]
    convert_element_type x2 -> x1, other arithmetic: 57.7 us -> 0.01 us  [body(): expert_ids.astype(jnp.float32)]
    sub x2 -> x0, matrix products: 38.2 us -> none  [doc_backward(): expo = jnp.exp(scores - top)]
    reduce_scatter x2 -> x4, waiting for transfers between devices: 74.2 us -> 41.5 us  [body(): lax.psum_scatter(mixed, 'row', scatter_dimension=0, tiled=True)]
    all_to_all x5 -> x9, starting transfers between devices: 26.5 us -> 51.7 us  [swap(): lax.all_to_all(blocks, ('section', 'col'), split_axis=0, concat_axis=0, t...]
    all_gather x2 -> x4, waiting for transfers between devices: 163 us -> 183 us  [body(): grads_line = lax.all_gather(row_grad, 'row', axis=0, tiled=False)]
  transfers between devices with their start and end apart: 13 -> 23, of which waited for: 9 -> 19; matrix products, arithmetic and copies ran while one was open for 31% -> 11% of each run, Pallas kernels for 11% -> 10%
where the time goes in v2:
time: 1280 us; the launch traced here: 1270 us
  waiting for transfers between devices  861 us (67%)
  matrix products  176 us (14%)
  Pallas kernels  122 us (10%)
  starting transfers between devices  58.3 us (5%)
  blocking collectives  15.2 us (1%)
  between operations  14 us (1%)
    all_to_all x9, waiting for transfers between devices, swap(): lax.all_to_all(blocks, ('section', 'col'), split_axis=0, concat_axis=0, t...  335 us
    reduce_scatter x4, waiting for transfers between devices, body(): lax.psum_scatter(term.astype(jnp.bfloat16), 'row', scatter_dimension=0, t...  290 us
    all_gather x4, waiting for transfers between devices, body(): grads_line = lax.all_gather(row_grad, 'row', axis=0, tiled=False)  183 us
    dot_general x4, matrix products, body(): lax.dot_general(grads_in, w_dn[:, lo:hi], (((1,), (1,)), ((), ())), prefe...  59.4 us
    pallas_call x1, Pallas kernels, attention_backward(): pl.pallas_call(doc_kernel, grid=(docs, heads), in_specs=[pl.BlockSpec((DO...  52.8 us
    all_to_all x9, starting transfers between devices, swap(): lax.all_to_all(blocks, ('section', 'col'), split_axis=0, concat_axis=0, t...  51.7 us
    dot_general x4, matrix products, body(): lax.dot_general(dgate_up, w_gu[lo:hi], (((1,), (1,)), ((), ())), preferre...  51 us
    pallas_call x5, Pallas kernels, pick_rows(): pl.pallas_call(pick_kernel, grid=(groups, width // part), in_specs=[pl.Bl...  43.8 us
  transfers between devices with their start and end apart: 23, of which 19 were waited for; matrix products, arithmetic and copies ran while one was open for 11% of the time, Pallas kernels for 10%

profile of v2, /device:TPU:0, one launch (start us, length us, event | category | flops | bytes accessed | tf_op | source)
XLA Modules:
  0.0 1266.0 jit_solution(340780463785357655)
XLA Ops:
  6.5 1.0 constant_dynamic-slice_fusion
  7.5 2.4 pad_maximum_fusion.2
  10.0 2.3 constant_dynamic-slice_fusion.2
  12.3 52.8 %doc_backward.1 = bf16[2048,1280]{1,0:T(8,128)(2,1)} custom-call(bf16[2048,1024]{1,0:T(8,128)(2,1)} %query_ref.1, bf16[2048,1024]{1,0:T(8,128)(2,1)} %grad_ref.1, bf16[2048,128]{1,0:T(8,128)(2,1)} %get-tuple-element.20.key_ref, bf16[2048,128]{1,0:T(8,128)(2,1)} %get-tuple-element.19.value_ref), custom_call_target="tpu_custom_call" | custom-call | flops 21474836480 | bytes 14680064 | tf_op jit(solution)/shard_map/doc_backward/pallas_call | solution.py:167
  65.0 9.1 all-gather.11.cloned.1.call-done
  74.1 7.1 convolution_convert_fusion.4
  81.3 7.3 convolution_convert_fusion.6
  88.7 15.2 %all-gather = f32[2048,16]{0,1:T(8,128)S(1)} all-gather(f32[512,16]{0,1:T(8,128)S(1)} %pad_maximum_fusion.3), channel_id=2, replica_groups=mesh['section'=2,'row'=4,'col'=4] {'row'}, dimensions={0}, use_global_device_ids=true | all-gather | bytes 163840 | tf_op jit(solution)/shard_map/all_gather | solution.py:223
  104.0 4.3 broadcast_in_dim.38
  108.3 5.6 all-to-all-start.4
  114.3 7.1 convolution_convert_fusion.7
  121.5 7.3 convolution_convert_fusion.5
  128.8 47.2 %reduce-scatter.15.cloned.1.call-done = bf16[512,512]{1,0:T(8,128)(2,1)} async-done(((bf16[2048,512]{1,0:T(8,128)(2,1)}), bf16[512,512]{1,0:T(8,128)(2,1)}) %reduce-scatter.15.cloned.1.call-update) | async-done | bytes 524304 | tf_op jit(solution)/shard_map/reduce_scatter | solution.py:275
  176.0 128.3 %reduce-scatter.11.cloned.1.call-done = bf16[512,512]{1,0:T(8,128)(2,1)} async-done(((bf16[2048,512]{1,0:T(8,128)(2,1)}), bf16[512,512]{1,0:T(8,128)(2,1)}) %reduce-scatter.11.cloned.1.call-update) | async-done | bytes 524304 | tf_op jit(solution)/shard_map/reduce_scatter | solution.py:275
  304.3 69.4 %reduce-scatter.9.cloned.1.call-done = bf16[512,512]{1,0:T(8,128)(2,1)} async-done(((bf16[2048,512]{1,0:T(8,128)(2,1)}), bf16[512,512]{1,0:T(8,128)(2,1)}) %reduce-scatter.9.cloned.1.call-update) | async-done | bytes 524304 | tf_op jit(solution)/shard_map/reduce_scatter | solution.py:275
  373.7 45.6 %reduce-scatter.13.cloned.1.call-done = bf16[512,512]{1,0:T(8,128)(2,1)} async-done(((bf16[2048,512]{1,0:T(8,128)(2,1)}), bf16[512,512]{1,0:T(8,128)(2,1)}) %reduce-scatter.13.cloned.1.call-update) | async-done | bytes 524304 | tf_op jit(solution)/shard_map/reduce_scatter | solution.py:275
  419.2 3.3 add_convert_fusion
  424.4 0.7 broadcast_in_dim.34.pos_ref
  425.1 42.6 %all-gather.17.cloned.1.call-done = bf16[2048,512]{1,0:T(8,128)(2,1)} async-done(((bf16[512,512]{1,0:T(8,128)(2,1)}), bf16[2048,512]{1,0:T(8,128)(2,1)}) %all-gather.17.cloned.1.call-update) | async-done | bytes 2097168 | tf_op jit(solution)/shard_map/all_gather | solution.py:280
  467.6 6.0 pick_rows.7
  473.6 4.6 all-to-all-start.2
  478.3 0.7 all-gather.13.cloned.1.call-update
  479.0 46.7 %all-gather.13.cloned.1.call-done = bf16[2048,512]{1,0:T(8,128)(2,1)} async-done(((bf16[512,512]{1,0:T(8,128)(2,1)}), bf16[2048,512]{1,0:T(8,128)(2,1)}) %all-gather.13.cloned.1.call-update) | async-done | bytes 2097168 | tf_op jit(solution)/shard_map/all_gather | solution.py:280
  525.7 6.0 pick_rows.5
  531.7 0.7 all-to-all-done.2
  532.4 4.6 all-to-all-start
  537.0 0.7 all-gather.15.cloned.1.call-update
  537.8 46.7 %all-gather.15.cloned.1.call-done = bf16[2048,512]{1,0:T(8,128)(2,1)} async-done(((bf16[512,512]{1,0:T(8,128)(2,1)}), bf16[2048,512]{1,0:T(8,128)(2,1)}) %all-gather.15.cloned.1.call-update) | async-done | bytes 2097168 | tf_op jit(solution)/shard_map/all_gather | solution.py:280
  584.5 6.0 pick_rows.6
  590.5 0.6 all-to-all-done
  591.1 4.6 all-to-all-start.1
  595.7 19.8 %pick_rows.9 = bf16[8,4,144,2048]{3,2,1,0:T(8,128)(2,1)} custom-call(s32[8,4,1,512]{3,2,1,0:T(1,128)} %broadcast_in_dim.34.pos_ref, bf16[4,512,2048]{2,1,0:T(8,128)(2,1)} %all-to-all-done.4.rows_ref), custom_call_target="tpu_custom_call" | custom-call | flops 9663676416 | bytes 27262976 | tf_op jit(solution)/shard_map/pick_rows/pallas_call | solution.py:45
  615.6 34.3 %all-to-all-done.1 = bf16[8,4,144,512]{3,2,1,0:T(8,128)(2,1)} async-done(((bf16[8,4,144,512]{3,2,1,0:T(8,128)(2,1)}), bf16[8,4,144,512]{3,2,1,0:T(8,128)(2,1)}, u32[]{:S(2)}, u32[]{:S(2)}) %all-to-all-start.1) | async-done | bytes 4718624 | tf_op jit(solution)/shard_map/all_to_all | solution.py:253
  649.9 5.9 all-to-all-start.5
  655.9 0.7 all-gather.19.cloned.1.call-update
  656.6 46.7 %all-gather.19.cloned.1.call-done = bf16[2048,512]{1,0:T(8,128)(2,1)} async-done(((bf16[512,512]{1,0:T(8,128)(2,1)}), bf16[2048,512]{1,0:T(8,128)(2,1)}) %all-gather.19.cloned.1.call-update) | async-done | bytes 2097168 | tf_op jit(solution)/shard_map/all_gather | solution.py:280
  703.3 6.0 pick_rows.8
  709.3 9.3 fusion.21
  718.6 9.4 fusion.25
  728.0 9.4 fusion.23
  737.4 124.2 %all-to-all-done.5 = bf16[8,4,144,2048]{3,2,1,0:T(8,128)(2,1)} async-done(((bf16[8,4,144,2048]{3,2,1,0:T(8,128)(2,1)}), bf16[8,4,144,2048]{3,2,1,0:T(8,128)(2,1)}, u32[]{:S(2)}, u32[]{:S(2)}) %all-to-all-start.5) | async-done | bytes 18874400 | tf_op jit(solution)/shard_map/all_to_all | solution.py:253
  861.6 13.1 %all-to-all-start.3 = ((bf16[8,4,144,512]{3,2,1,0:T(8,128)(2,1)}), bf16[8,4,144,512]{3,2,1,0:T(8,128)(2,1)}, u32[]{:S(2)}, u32[]{:S(2)}) async-start(bf16[8,4,144,512]{3,2,1,0:T(8,128)(2,1)} %pick_rows.8), calls=%async_computation.7 | async-start | bytes 9437184 | tf_op jit(solution)/shard_map/all_to_all | solution.py:253
  874.7 36.7 %fusion.3 = f32[4608,1536]{0,1:T(8,128)} fusion(bf16[4608,2048]{1,0:T(8,128)(2,1)} %bitcast.10, bf16[1,2048,1536]{2,1,0:T(8,128)(2,1)} %param.24), kind=kOutput, calls=%fused_computation.12 | convolution fusion | flops 28991029248 | bytes 53477376 | tf_op jit(solution)/shard_map/dot_general | solution.py:261
  911.5 17.1 %all-to-all-done.3 = bf16[8,4,144,512]{3,2,1,0:T(8,128)(2,1)} async-done(((bf16[8,4,144,512]{3,2,1,0:T(8,128)(2,1)}), bf16[8,4,144,512]{3,2,1,0:T(8,128)(2,1)}, u32[]{:S(2)}, u32[]{:S(2)}) %all-to-all-start.3) | async-done | bytes 4718624 | tf_op jit(solution)/shard_map/all_to_all | solution.py:253
  928.6 31.3 %fusion.2 = (bf16[4608,768]{0,1:T(8,128)(2,1)}, bf16[4608,768]{0,1:T(8,128)(2,1)}) fusion(f32[4608,1536]{0,1:T(8,128)} %fusion.3, bf16[4608,512]{1,0:T(8,128)(2,1)} %bitcast.9, bf16[768,2048]{1,0:T(8,128)(2,1)S(1)} %bitcast.51, f32[4608,768]{0,1:T(8,128)} %fusion.21, f32[4608,768]{0,1:T(8,128)} %fusion.25, f32[4608,768]{0,1:T(8,128)} %fusion.23), kind=kOutput, calls=%fused_computation.3 | convolution fusion | flops 3680501760 | bytes 90439680 | tf_op jit(solution)/shard_map/dot_general | solution.py:282
  959.9 12.8 %convolution_convert_fusion = bf16[4608,512]{1,0:T(8,128)(2,1)} fusion(bf16[1,2048,1536]{2,1,0:T(8,128)(2,1)} %param.24, bf16[4608,768]{0,1:T(8,128)(2,1)} %get-tuple-element.10, bf16[4608,768]{0,1:T(8,128)(2,1)} %get-tuple-element.9), kind=kOutput, calls=%fused_computation.8 | convolution fusion | flops 7278428160 | bytes 20447232 | tf_op jit(solution)/shard_map/dot_general | solution.py:300
  972.7 5.0 all-to-all-start.9
  977.9 0.7 broadcast_in_dim.37.weight_ref
  978.6 12.8 %convolution_convert_fusion.1 = bf16[4608,512]{1,0:T(8,128)(2,1)} fusion(bf16[1,2048,1536]{2,1,0:T(8,128)(2,1)} %param.24, bf16[4608,768]{0,1:T(8,128)(2,1)} %get-tuple-element.10, bf16[4608,768]{0,1:T(8,128)(2,1)} %get-tuple-element.9), kind=kOutput, calls=%fused_computation.9 | convolution fusion | flops 7278428160 | bytes 20447232 | tf_op jit(solution)/shard_map/dot_general | solution.py:300
  991.4 40.4 %all-to-all-done.9.rows_ref = bf16[8,4,144,512]{3,2,1,0:T(8,128)(2,1)} async-done(((bf16[8,4,144,512]{3,2,1,0:T(8,128)(2,1)}), bf16[8,4,144,512]{3,2,1,0:T(8,128)(2,1)}, u32[]{:S(2)}, u32[]{:S(2)}) %all-to-all-start.9) | async-done | bytes 4718624 | tf_op jit(solution)/shard_map/all_to_all | solution.py:253
  1031.8 4.6 all-to-all-start.8
  1036.5 6.4 mix_rows.7
  1042.9 12.8 %convolution_convert_fusion.2 = bf16[4608,512]{1,0:T(8,128)(2,1)} fusion(bf16[1,2048,1536]{2,1,0:T(8,128)(2,1)} %param.24, bf16[4608,768]{0,1:T(8,128)(2,1)} %get-tuple-element.10, bf16[4608,768]{0,1:T(8,128)(2,1)} %get-tuple-element.9), kind=kOutput, calls=%fused_computation.10 | convolution fusion | flops 7278428160 | bytes 20447232 | tf_op jit(solution)/shard_map/dot_general | solution.py:300
  1055.6 34.9 %all-to-all-done.8.rows_ref = bf16[8,4,144,512]{3,2,1,0:T(8,128)(2,1)} async-done(((bf16[8,4,144,512]{3,2,1,0:T(8,128)(2,1)}), bf16[8,4,144,512]{3,2,1,0:T(8,128)(2,1)}, u32[]{:S(2)}, u32[]{:S(2)}) %all-to-all-start.8) | async-done | bytes 4718624 | tf_op jit(solution)/shard_map/all_to_all | solution.py:253
  1090.5 4.6 all-to-all-start.7
  1095.4 6.4 mix_rows.6
  1101.9 12.7 %convolution_convert_fusion.3 = bf16[4608,512]{1,0:T(8,128)(2,1)} fusion(bf16[1,2048,1536]{2,1,0:T(8,128)(2,1)} %param.24, bf16[4608,768]{0,1:T(8,128)(2,1)} %get-tuple-element.10, bf16[4608,768]{0,1:T(8,128)(2,1)} %get-tuple-element.9), kind=kOutput, calls=%fused_computation.11 | convolution fusion | flops 7278428160 | bytes 20447232 | tf_op jit(solution)/shard_map/dot_general | solution.py:300
  1114.6 34.6 %all-to-all-done.7.rows_ref = bf16[8,4,144,512]{3,2,1,0:T(8,128)(2,1)} async-done(((bf16[8,4,144,512]{3,2,1,0:T(8,128)(2,1)}), bf16[8,4,144,512]{3,2,1,0:T(8,128)(2,1)}, u32[]{:S(2)}, u32[]{:S(2)}) %all-to-all-start.7) | async-done | bytes 4718624 | tf_op jit(solution)/shard_map/all_to_all | solution.py:253
  1149.3 4.6 all-to-all-start.6
  1153.9 6.4 mix_rows.5
  1160.4 47.6 %all-to-all-done.6.rows_ref = bf16[8,4,144,512]{3,2,1,0:T(8,128)(2,1)} async-done(((bf16[8,4,144,512]{3,2,1,0:T(8,128)(2,1)}), bf16[8,4,144,512]{3,2,1,0:T(8,128)(2,1)}, u32[]{:S(2)}, u32[]{:S(2)}) %all-to-all-start.6) | async-done | bytes 4718624 | tf_op jit(solution)/shard_map/all_to_all | solution.py:253
  1208.0 6.4 mix_rows.4
  1214.5 41.5 %reduce-scatter.17.cloned.1.call-done = bf16[512,512]{1,0:T(8,128)(2,1)} async-done(((bf16[2048,512]{1,0:T(8,128)(2,1)}), bf16[512,512]{1,0:T(8,128)(2,1)}) %reduce-scatter.17.cloned.1.call-update) | async-done | bytes 524304 | tf_op jit(solution)/shard_map/reduce_scatter | solution.py:308
  1256.0 3.1 pad_maximum_fusion.1
  (56 shorter events, 3.4 us)
Async XLA Ops:
  6.5 67.6 %all-gather.11.cloned.1.call-start = ((), (), s32[]{:S(2)}) async-start(), calls=%async_computation.18 | async-start | bytes 6553600 | tf_op jit(solution)/shard_map/all_gather | solution.py:212
  9.9 166.1 %reduce-scatter.15.cloned.1.call-start = ((), (), s32[]{:S(2)}) async-start(), calls=%async_computation.22 | async-start | bytes 2621440 | tf_op jit(solution)/shard_map/reduce_scatter | solution.py:275
  81.3 7.4 copy-start.5
  81.3 7.4 copy-start.6
  81.3 22.7 %copy-start = (bf16[512,2048]{1,0:T(8,128)(2,1)S(1)}, bf16[512,2048]{1,0:T(8,128)(2,1)}, u32[]{:S(2)}) copy-start(bf16[512,2048]{1,0:T(8,128)(2,1)} %param.21) | copy-start | bytes 6291460
  81.3 223.0 %reduce-scatter.11.cloned.1.call-start = ((), (), s32[]{:S(2)}) async-start(), calls=%async_computation.20 | async-start | bytes 2621440 | tf_op jit(solution)/shard_map/reduce_scatter | solution.py:275
  108.3 365.3 %all-to-all-start.4 = ((bf16[4,512,2048]{2,1,0:T(8,128)(2,1)}), bf16[4,512,2048]{2,1,0:T(8,128)(2,1)}, u32[]{:S(2)}, u32[]{:S(2)}) async-start(bf16[4,512,2048]{2,1,0:T(8,128)(2,1)} %broadcast_in_dim.38), calls=%async_computation.8 | async-start | bytes 16777216 | tf_op jit(solution)/shard_map/all_to_all | solution.py:227
  114.0 259.7 %reduce-scatter.9.cloned.1.call-start = ((), (), s32[]{:S(2)}) async-start(), calls=%async_computation.19 | async-start | bytes 2621440 | tf_op jit(solution)/shard_map/reduce_scatter | solution.py:275
  121.4 297.8 %copy-start.1 = (bf16[512,2048]{1,0:T(8,128)(2,1)S(1)}, bf16[512,2048]{1,0:T(8,128)(2,1)}, u32[]{:S(2)}) copy-start(bf16[512,2048]{1,0:T(8,128)(2,1)} %param.20) | copy-start | bytes 6291460
  121.4 297.8 %reduce-scatter.13.cloned.1.call-start = ((), (), s32[]{:S(2)}) async-start(), calls=%async_computation.21 | async-start | bytes 2621440 | tf_op jit(solution)/shard_map/reduce_scatter | solution.py:275
  128.8 338.9 %all-gather.17.cloned.1.call-start = ((), (), s32[]{:S(2)}) async-start(), calls=%async_computation.29 | async-start | bytes 2621440 | tf_op jit(solution)/shard_map/all_gather | solution.py:280
  422.7 1.7 copy-start.7
  423.3 0.6 copy-start.2
  473.6 58.7 %all-to-all-start.2 = ((bf16[8,4,144,512]{3,2,1,0:T(8,128)(2,1)}), bf16[8,4,144,512]{3,2,1,0:T(8,128)(2,1)}, u32[]{:S(2)}, u32[]{:S(2)}) async-start(bf16[8,4,144,512]{3,2,1,0:T(8,128)(2,1)} %pick_rows.7), calls=%async_computation.5 | async-start | bytes 9437184 | tf_op jit(solution)/shard_map/all_to_all | solution.py:253
  478.3 47.5 %all-gather.13.cloned.1.call-start = ((), (), s32[]{:S(2)}) async-start(), calls=%async_computation.27 | async-start | bytes 2621440 | tf_op jit(solution)/shard_map/all_gather | solution.py:280
  532.4 58.7 %all-to-all-start = ((bf16[8,4,144,512]{3,2,1,0:T(8,128)(2,1)}), bf16[8,4,144,512]{3,2,1,0:T(8,128)(2,1)}, u32[]{:S(2)}, u32[]{:S(2)}) async-start(bf16[8,4,144,512]{3,2,1,0:T(8,128)(2,1)} %pick_rows.5), calls=%async_computation.1 | async-start | bytes 9437184 | tf_op jit(solution)/shard_map/all_to_all | solution.py:253
  537.0 47.5 %all-gather.15.cloned.1.call-start = ((), (), s32[]{:S(2)}) async-start(), calls=%async_computation.28 | async-start | bytes 2621440 | tf_op jit(solution)/shard_map/all_gather | solution.py:280
  591.1 58.8 %all-to-all-start.1 = ((bf16[8,4,144,512]{3,2,1,0:T(8,128)(2,1)}), bf16[8,4,144,512]{3,2,1,0:T(8,128)(2,1)}, u32[]{:S(2)}, u32[]{:S(2)}) async-start(bf16[8,4,144,512]{3,2,1,0:T(8,128)(2,1)} %pick_rows.6), calls=%async_computation.3 | async-start | bytes 9437184 | tf_op jit(solution)/shard_map/all_to_all | solution.py:253
  649.9 211.7 %all-to-all-start.5 = ((bf16[8,4,144,2048]{3,2,1,0:T(8,128)(2,1)}), bf16[8,4,144,2048]{3,2,1,0:T(8,128)(2,1)}, u32[]{:S(2)}, u32[]{:S(2)}) async-start(bf16[8,4,144,2048]{3,2,1,0:T(8,128)(2,1)} %pick_rows.9), calls=%async_computation.9 | async-start | bytes 37748736 | tf_op jit(solution)/shard_map/all_to_all | solution.py:253
  655.8 53.5 %copy-start.9 = (bf16[1,768,2048]{2,1,0:T(8,128)(2,1)S(1)}, bf16[1,768,2048]{2,1,0:T(8,128)(2,1)}, u32[]{:S(2)}) copy-start(bf16[1,768,2048]{2,1,0:T(8,128)(2,1)} %param.25) | copy-start | bytes 9437188
  655.8 47.4 %all-gather.19.cloned.1.call-start = ((), (), s32[]{:S(2)}) async-start(), calls=%async_computation.30 | async-start | bytes 2621440 | tf_op jit(solution)/shard_map/all_gather | solution.py:280
  861.6 67.0 %all-to-all-start.3 = ((bf16[8,4,144,512]{3,2,1,0:T(8,128)(2,1)}), bf16[8,4,144,512]{3,2,1,0:T(8,128)(2,1)}, u32[]{:S(2)}, u32[]{:S(2)}) async-start(bf16[8,4,144,512]{3,2,1,0:T(8,128)(2,1)} %pick_rows.8), calls=%async_computation.7 | async-start | bytes 9437184 | tf_op jit(solution)/shard_map/all_to_all | solution.py:253
  972.7 5.0 copy-start.3
  972.7 5.0 copy-start.4
  972.7 5.0 copy-start.8
  972.7 59.1 %all-to-all-start.9 = ((bf16[8,4,144,512]{3,2,1,0:T(8,128)(2,1)}), bf16[8,4,144,512]{3,2,1,0:T(8,128)(2,1)}, u32[]{:S(2)}, u32[]{:S(2)}) async-start(bf16[8,4,144,512]{3,2,1,0:T(8,128)(2,1)} %bitcast.47), calls=%async_computation.16 | async-start | bytes 9437184 | tf_op jit(solution)/shard_map/all_to_all | solution.py:253
  1031.8 58.8 %all-to-all-start.8 = ((bf16[8,4,144,512]{3,2,1,0:T(8,128)(2,1)}), bf16[8,4,144,512]{3,2,1,0:T(8,128)(2,1)}, u32[]{:S(2)}, u32[]{:S(2)}) async-start(bf16[8,4,144,512]{3,2,1,0:T(8,128)(2,1)} %bitcast.46), calls=%async_computation.14 | async-start | bytes 9437184 | tf_op jit(solution)/shard_map/all_to_all | solution.py:253
  1036.4 178.0 %reduce-scatter.23.cloned.1.call-start = ((), (), s32[]{:S(2)}) async-start(), calls=%async_computation.26 | async-start | bytes 2621440 | tf_op jit(solution)/shard_map/reduce_scatter | solution.py:308
  1090.5 58.7 %all-to-all-start.7 = ((bf16[8,4,144,512]{3,2,1,0:T(8,128)(2,1)}), bf16[8,4,144,512]{3,2,1,0:T(8,128)(2,1)}, u32[]{:S(2)}, u32[]{:S(2)}) async-start(bf16[8,4,144,512]{3,2,1,0:T(8,128)(2,1)} %bitcast.45), calls=%async_computation.12 | async-start | bytes 9437184 | tf_op jit(solution)/shard_map/all_to_all | solution.py:253
  1095.1 119.3 %reduce-scatter.21.cloned.1.call-start = ((), (), s32[]{:S(2)}) async-start(), calls=%async_computation.25 | async-start | bytes 2621440 | tf_op jit(solution)/shard_map/reduce_scatter | solution.py:308
  1149.3 58.8 %all-to-all-start.6 = ((bf16[8,4,144,512]{3,2,1,0:T(8,128)(2,1)}), bf16[8,4,144,512]{3,2,1,0:T(8,128)(2,1)}, u32[]{:S(2)}, u32[]{:S(2)}) async-start(bf16[8,4,144,512]{3,2,1,0:T(8,128)(2,1)} %bitcast.44), calls=%async_computation.10 | async-start | bytes 9437184 | tf_op jit(solution)/shard_map/all_to_all | solution.py:253
  1153.9 60.6 %reduce-scatter.19.cloned.1.call-start = ((), (), s32[]{:S(2)}) async-start(), calls=%async_computation.24 | async-start | bytes 2621440 | tf_op jit(solution)/shard_map/reduce_scatter | solution.py:308
  1160.3 95.6 %reduce-scatter.17.cloned.1.call-start = ((), (), s32[]{:S(2)}) async-start(), calls=%async_computation.23 | async-start | bytes 2621440 | tf_op jit(solution)/shard_map/reduce_scatter | solution.py:308
Sparse Core Ops, SparseCore 0:
  10.1 64.0 all-gather.10
  81.4 94.5 reduce-scatter.14
  178.3 125.9 reduce-scatter.10
  306.4 67.2 reduce-scatter.8
  375.8 43.3 reduce-scatter.12
  422.7 44.8 all-gather.16
  480.6 45.0 all-gather.12
  539.4 45.0 all-gather.14
  658.2 45.0 all-gather.18
  1043.0 42.9 reduce-scatter.22
  1102.0 42.9 reduce-scatter.20
  1160.5 42.9 reduce-scatter.18
  1214.5 41.3 reduce-scatter.16

commit v3 on v2

--- a/solution.py
+++ b/solution.py
@@ -10,7 +10,7 @@
 HEAD_DIM = 128
 TOPK = 8
 DOC = 1024
-CHUNKS = 4
+CHUNKS = 2
 PART = 512
 ATT_BLOCK = 256
 LOG2_E = 1.4426950408889634
@@ -221,7 +221,7 @@
 
     routes = jnp.concatenate([expert_ids.astype(jnp.float32), route_weights], axis=1)
     routes_line = lax.all_gather(routes, "row", axis=0, tiled=False)
-    routes_line, moe_input = lax.optimization_barrier((routes_line, moe_input))
+    routes_line, moe_input, queries = lax.optimization_barrier((routes_line, moe_input, queries))
     ids_line = routes_line[..., :TOPK].astype(jnp.int32)
     weights_line = routes_line[..., TOPK:]
     rows_line = lax.all_to_all(
@@ -257,7 +257,9 @@
     w_gu = w_gate_up[0]
     w_dn = w_down[0]
     ff = w_dn.shape[0]
-    rows_in = swap(pick_rows(pos, rows_line, capacity)).reshape(-1, model)
+    rows_in = swap(pick_rows(pos, rows_line, capacity))
+    rows_in, pos_grads = lax.optimization_barrier((rows_in, pos))
+    rows_in = rows_in.reshape(-1, model)
     gate_up = jnp.dot(rows_in, w_gu, preferred_element_type=jnp.float32)
 
     dqkv = attention_backward(queries, out_grad, key_head, value_head)
@@ -278,7 +280,7 @@
         layer_grad = head_grad + resid_grad[:, lo:hi].astype(jnp.float32)
         row_grad = layer_grad.astype(jnp.bfloat16)
         grads_line = lax.all_gather(row_grad, "row", axis=0, tiled=False)
-        grads_in = swap(pick_rows(pos, grads_line, capacity)).reshape(-1, span)
+        grads_in = swap(pick_rows(pos_grads, grads_line, capacity)).reshape(-1, span)
         piece = lax.dot_general(
             grads_in,
             w_dn[:, lo:hi],

time: 1280 us -> 1130 us (0.88)
  waiting for transfers between devices: 861 us -> 771 us
  matrix products: 176 us -> 149 us
  starting transfers between devices: 58.3 us -> 32.4 us
    reduce_scatter x4 -> x2, waiting for transfers between devices: 290 us -> 76.1 us  [body(): lax.psum_scatter(term.astype(jnp.bfloat16), 'row', scatter_dimension=0, t...]
    all_to_all x1, waiting for transfers between devices: 0.01 us -> 181 us  [body(): lax.all_to_all(jnp.broadcast_to(moe_input[None], (row_count,) + moe_input...]
    all_gather x4 -> x2, waiting for transfers between devices: 183 us -> 81.7 us  [body(): grads_line = lax.all_gather(row_grad, 'row', axis=0, tiled=False)]
    reduce_scatter x4 -> x2, waiting for transfers between devices: 41.5 us -> 74.7 us  [body(): lax.psum_scatter(mixed, 'row', scatter_dimension=0, tiled=True)]
    all_to_all x9 -> x5, starting transfers between devices: 51.7 us -> 26.3 us  [swap(): lax.all_to_all(blocks, ('section', 'col'), split_axis=0, concat_axis=0, t...]
    all_to_all x9 -> x5, waiting for transfers between devices: 335 us -> 357 us  [swap(): lax.all_to_all(blocks, ('section', 'col'), split_axis=0, concat_axis=0, t...]
    dot_general x4 -> x2, matrix products: 59.4 us -> 41.8 us  [body(): lax.dot_general(grads_in, w_dn[:, lo:hi], (((1,), (1,)), ((), ())), prefe...]
    dot_general x4 -> x2, matrix products: 28.8 us -> 20.4 us  [body(): lax.dot_general(dqkv, wcat_whole[lo:hi], (((1,), (1,)), ((), ())), prefer...]
  transfers between devices with their start and end apart: 23 -> 13, of which waited for: 19 -> 9; matrix products, arithmetic and copies ran while one was open for 11% -> 9% of each run, Pallas kernels for 10% -> 9%
where the time goes in v3:
time: 1130 us; the launch traced here: 1120 us
  waiting for transfers between devices  771 us (68%)
  matrix products  149 us (13%)
  Pallas kernels  116 us (10%)
  starting transfers between devices  32.4 us (3%)
  blocking collectives  15.1 us (1%)
  between operations  13.9 us (1%)
  other arithmetic  12 us (1%)
    all_to_all x5, waiting for transfers between devices, swap(): lax.all_to_all(blocks, ('section', 'col'), split_axis=0, concat_axis=0, t...  357 us
    all_to_all x1, waiting for transfers between devices, body(): lax.all_to_all(jnp.broadcast_to(moe_input[None], (row_count,) + moe_input...  181 us
    all_gather x2, waiting for transfers between devices, body(): grads_line = lax.all_gather(row_grad, 'row', axis=0, tiled=False)  81.7 us
    reduce_scatter x2, waiting for transfers between devices, body(): lax.psum_scatter(term.astype(jnp.bfloat16), 'row', scatter_dimension=0, t...  76.1 us
    reduce_scatter x2, waiting for transfers between devices, body(): lax.psum_scatter(mixed, 'row', scatter_dimension=0, tiled=True)  74.7 us
    pallas_call x1, Pallas kernels, attention_backward(): pl.pallas_call(doc_kernel, grid=(docs, heads), in_specs=[pl.BlockSpec((DO...  52.7 us
    dot_general x2, matrix products, body(): lax.dot_general(dgate_up, w_gu[lo:hi], (((1,), (1,)), ((), ())), preferre...  50 us
    dot_general x2, matrix products, body(): lax.dot_general(grads_in, w_dn[:, lo:hi], (((1,), (1,)), ((), ())), prefe...  41.8 us
  transfers between devices with their start and end apart: 13, of which 9 were waited for; matrix products, arithmetic and copies ran while one was open for 9% of the time, Pallas kernels for 9%

profile of v3, /device:TPU:0, one launch (start us, length us, event | category | flops | bytes accessed | tf_op | source)
XLA Modules:
  0.0 1120.1 jit_solution(18007493178758037779)
XLA Ops:
  6.5 0.0 all-gather.7.cloned.1.call-start
  6.5 1.1 constant_dynamic-slice_fusion
  7.7 2.4 pad_maximum_fusion.4
  10.1 0.0 all-gather.7.cloned.1.call-update
  10.1 0.7 convert_element_type.42
  10.8 0.7 pad_maximum_fusion.5
  11.5 15.1 %all-gather = f32[2048,16]{0,1:T(8,128)S(1)} all-gather(f32[512,16]{0,1:T(8,128)S(1)} %pad_maximum_fusion.5), channel_id=2, replica_groups=mesh['section'=2,'row'=4,'col'=4] {'row'}, dimensions={0}, use_global_device_ids=true | all-gather | bytes 163840 | tf_op jit(solution)/shard_map/all_gather | solution.py:223
  26.6 0.1 reshape.53
  26.7 4.3 broadcast_in_dim.38
  31.1 5.6 all-to-all-start
  36.7 0.0 reduce-scatter.7.cloned.1.call-start
  36.7 2.4 constant_dynamic-slice_fusion.2
  39.1 52.7 %doc_backward.1 = bf16[2048,1280]{1,0:T(8,128)(2,1)} custom-call(bf16[2048,1024]{1,0:T(8,128)(2,1)} %query_ref, bf16[2048,1024]{1,0:T(8,128)(2,1)} %grad_ref.1, bf16[2048,128]{1,0:T(8,128)(2,1)} %get-tuple-element.24.key_ref, bf16[2048,128]{1,0:T(8,128)(2,1)} %get-tuple-element.23.value_ref), custom_call_target="tpu_custom_call" | custom-call | flops 21474836480 | bytes 14680064 | tf_op jit(solution)/shard_map/doc_backward/pallas_call | solution.py:167
  91.8 10.1 convolution_convert_fusion.2
  101.9 0.0 reduce-scatter.7.cloned.1.call-update
  102.0 0.6 fusion.24
  102.7 0.6 copy-done.2
  103.3 0.2 compare_reduce_fusion
  103.5 0.2 fusion.14
  103.8 0.0 copy-done.5
  103.8 0.7 broadcast_in_dim.34.pos_ref
  104.5 180.7 %all-to-all-done.rows_ref = bf16[4,512,2048]{2,1,0:T(8,128)(2,1)} async-done(((bf16[4,512,2048]{2,1,0:T(8,128)(2,1)}), bf16[4,512,2048]{2,1,0:T(8,128)(2,1)}, u32[]{:S(2)}, u32[]{:S(2)}) %all-to-all-start) | async-done | bytes 8388640 | tf_op jit(solution)/shard_map/all_to_all | solution.py:227
  285.1 19.7 %pick_rows.3 = bf16[8,4,144,2048]{3,2,1,0:T(8,128)(2,1)} custom-call(s32[8,4,1,512]{3,2,1,0:T(1,128)} %broadcast_in_dim.34.pos_ref, bf16[4,512,2048]{2,1,0:T(8,128)(2,1)} %all-to-all-done.rows_ref), custom_call_target="tpu_custom_call" | custom-call | flops 9663676416 | bytes 27262976 | tf_op jit(solution)/shard_map/pick_rows/pallas_call | solution.py:45
  304.9 6.0 all-to-all-start.1
  310.8 0.0 copy-start.1
  310.8 0.0 reduce-scatter.5.cloned.1.call-start
  310.9 10.3 convolution_convert_fusion.3
  321.2 0.0 reduce-scatter.5.cloned.1.call-update
  321.2 0.3 all-gather.9.cloned.1.call-start
  321.5 0.0 reduce-scatter.7.cloned.1.call-done
  321.5 76.0 %reduce-scatter.5.cloned.1.call-done = bf16[512,1024]{1,0:T(8,128)(2,1)} async-done(((bf16[2048,1024]{1,0:T(8,128)(2,1)}), bf16[512,1024]{1,0:T(8,128)(2,1)}) %reduce-scatter.5.cloned.1.call-update) | async-done | bytes 1048592 | tf_op jit(solution)/shard_map/reduce_scatter | solution.py:277
  397.6 3.9 add_convert_fusion
  401.5 0.0 all-gather.9.cloned.1.call-update
  401.5 115.1 %all-to-all-done.1 = bf16[8,4,144,2048]{3,2,1,0:T(8,128)(2,1)} async-done(((bf16[8,4,144,2048]{3,2,1,0:T(8,128)(2,1)}), bf16[8,4,144,2048]{3,2,1,0:T(8,128)(2,1)}, u32[]{:S(2)}, u32[]{:S(2)}) %all-to-all-start.1) | async-done | bytes 18874400 | tf_op jit(solution)/shard_map/all_to_all | solution.py:253
  516.6 10.5 pick_rows.4
  527.2 5.0 all-to-all-start.2
  532.2 0.0 all-gather.11.cloned.1.call-start
  532.3 0.5 all-gather.11.cloned.1.call-update
  532.8 81.7 %all-gather.11.cloned.1.call-done = bf16[2048,1024]{1,0:T(8,128)(2,1)} async-done(((bf16[512,1024]{1,0:T(8,128)(2,1)}), bf16[2048,1024]{1,0:T(8,128)(2,1)}) %all-gather.11.cloned.1.call-update) | async-done | bytes 4194320 | tf_op jit(solution)/shard_map/all_gather | solution.py:282
  614.5 10.6 pick_rows.5
  625.1 11.8 %all-to-all-done.2 = bf16[8,4,144,1024]{3,2,1,0:T(8,128)(2,1)} async-done(((bf16[8,4,144,1024]{3,2,1,0:T(8,128)(2,1)}), bf16[8,4,144,1024]{3,2,1,0:T(8,128)(2,1)}, u32[]{:S(2)}, u32[]{:S(2)}) %all-to-all-start.2) | async-done | bytes 9437216 | tf_op jit(solution)/shard_map/all_to_all | solution.py:253
  636.9 5.0 all-to-all-start.3
  641.9 0.0 copy-start.7
  642.0 36.8 %fusion.3 = f32[4608,1536]{0,1:T(8,128)} fusion(bf16[4608,2048]{1,0:T(8,128)(2,1)} %bitcast.6, bf16[1,2048,1536]{2,1,0:T(8,128)(2,1)} %param.24), kind=kOutput, calls=%fused_computation.10 | convolution fusion | flops 28991029248 | bytes 53477376 | tf_op jit(solution)/shard_map/dot_general | solution.py:263
  678.8 13.8 %fusion.12 = f32[4608,768]{0,1:T(8,128)} fusion(bf16[4608,1024]{1,0:T(8,128)(2,1)} %bitcast.2, bf16[768,2048]{1,0:T(8,128)(2,1)S(1)} %bitcast.32), kind=kOutput, calls=%fused_computation.24 | convolution fusion | flops 7247757312 | bytes 25165824 | tf_op jit(solution)/shard_map/dot_general | solution.py:284
  692.6 54.1 %all-to-all-done.3 = bf16[8,4,144,1024]{3,2,1,0:T(8,128)(2,1)} async-done(((bf16[8,4,144,1024]{3,2,1,0:T(8,128)(2,1)}), bf16[8,4,144,1024]{3,2,1,0:T(8,128)(2,1)}, u32[]{:S(2)}, u32[]{:S(2)}) %all-to-all-start.3) | async-done | bytes 9437216 | tf_op jit(solution)/shard_map/all_to_all | solution.py:253
  746.6 28.1 %fusion.2 = (bf16[4608,768]{0,1:T(8,128)(2,1)}, bf16[4608,768]{0,1:T(8,128)(2,1)}) fusion(f32[4608,1536]{0,1:T(8,128)} %fusion.3, f32[4608,768]{0,1:T(8,128)} %fusion.12, bf16[4608,1024]{1,0:T(8,128)(2,1)} %bitcast.5, bf16[768,2048]{1,0:T(8,128)(2,1)S(1)} %bitcast.33), kind=kOutput, calls=%fused_computation.3 | convolution fusion | flops 7297302528 | bytes 67633152 | tf_op jit(solution)/shard_map/dot_general | solution.py:284
  774.7 29.5 %convolution_convert_fusion = bf16[4608,1024]{1,0:T(8,128)(2,1)} fusion(bf16[4608,768]{0,1:T(8,128)(2,1)} %get-tuple-element.16, bf16[4608,768]{0,1:T(8,128)(2,1)} %get-tuple-element.15, bf16[1,2048,1536]{2,1,0:T(8,128)(2,1)} %param.24), kind=kOutput, calls=%fused_computation.7 | convolution fusion | flops 14528544768 | bytes 26738688 | tf_op jit(solution)/shard_map/dot_general | solution.py:302
  804.2 5.2 all-to-all-start.5
  809.5 0.2 fusion.17
  809.7 0.7 broadcast_in_dim.37.weight_ref
  810.4 20.5 %convolution_convert_fusion.1 = bf16[4608,1024]{1,0:T(8,128)(2,1)} fusion(bf16[4608,768]{0,1:T(8,128)(2,1)} %get-tuple-element.16, bf16[4608,768]{0,1:T(8,128)(2,1)} %get-tuple-element.15, bf16[1,2048,1536]{2,1,0:T(8,128)(2,1)} %param.24), kind=kOutput, calls=%fused_computation.8 | convolution fusion | flops 14528544768 | bytes 26738688 | tf_op jit(solution)/shard_map/dot_general | solution.py:302
  830.8 83.3 %all-to-all-done.5.rows_ref = bf16[8,4,144,1024]{3,2,1,0:T(8,128)(2,1)} async-done(((bf16[8,4,144,1024]{3,2,1,0:T(8,128)(2,1)}), bf16[8,4,144,1024]{3,2,1,0:T(8,128)(2,1)}, u32[]{:S(2)}, u32[]{:S(2)}) %all-to-all-start.5) | async-done | bytes 9437216 | tf_op jit(solution)/shard_map/all_to_all | solution.py:253
  914.1 5.1 all-to-all-start.4
  919.2 0.0 reduce-scatter.11.cloned.1.call-start
  919.2 11.4 %mix_rows.3 = bf16[2048,1024]{1,0:T(8,128)(2,1)} custom-call(s32[8,4,1,512]{3,2,1,0:T(1,128)} %broadcast_in_dim.34.pos_ref, f32[8,4,1,512]{3,2,1,0:T(1,128)} %broadcast_in_dim.37.weight_ref, bf16[8,4,144,1024]{3,2,1,0:T(8,128)(2,1)} %all-to-all-done.5.rows_ref), custom_call_target="tpu_custom_call" | custom-call | flops 4831838208 | bytes 13631488 | tf_op jit(solution)/shard_map/mix_rows/pallas_call | solution.py:90
  930.6 0.0 reduce-scatter.11.cloned.1.call-update
  930.7 0.0 reduce-scatter.9.cloned.1.call-start
  930.7 93.2 %all-to-all-done.4.rows_ref = bf16[8,4,144,1024]{3,2,1,0:T(8,128)(2,1)} async-done(((bf16[8,4,144,1024]{3,2,1,0:T(8,128)(2,1)}), bf16[8,4,144,1024]{3,2,1,0:T(8,128)(2,1)}, u32[]{:S(2)}, u32[]{:S(2)}) %all-to-all-start.4) | async-done | bytes 9437216 | tf_op jit(solution)/shard_map/all_to_all | solution.py:253
  1023.9 11.4 %mix_rows.2 = bf16[2048,1024]{1,0:T(8,128)(2,1)} custom-call(s32[8,4,1,512]{3,2,1,0:T(1,128)} %broadcast_in_dim.34.pos_ref, f32[8,4,1,512]{3,2,1,0:T(1,128)} %broadcast_in_dim.37.weight_ref, bf16[8,4,144,1024]{3,2,1,0:T(8,128)(2,1)} %all-to-all-done.4.rows_ref), custom_call_target="tpu_custom_call" | custom-call | flops 4831838208 | bytes 13631488 | tf_op jit(solution)/shard_map/mix_rows/pallas_call | solution.py:90
  1035.2 0.0 reduce-scatter.9.cloned.1.call-update
  1035.2 0.0 reduce-scatter.11.cloned.1.call-done
  1035.3 74.7 %reduce-scatter.9.cloned.1.call-done = bf16[512,1024]{1,0:T(8,128)(2,1)} async-done(((bf16[2048,1024]{1,0:T(8,128)(2,1)}), bf16[512,1024]{1,0:T(8,128)(2,1)}) %reduce-scatter.9.cloned.1.call-update) | async-done | bytes 1048592 | tf_op jit(solution)/shard_map/reduce_scatter | solution.py:310
  1110.0 3.1 pad_maximum_fusion.3
  (16 shorter events, 0.1 us)
Async XLA Ops:
  6.5 20.2 %copy-start = (bf16[512,2048]{1,0:T(8,128)(2,1)S(1)}, bf16[512,2048]{1,0:T(8,128)(2,1)}, u32[]{:S(2)}) copy-start(bf16[512,2048]{1,0:T(8,128)(2,1)} %param.21) | copy-start | bytes 6291460
  6.5 85.3 %all-gather.7.cloned.1.call-start = ((), (), s32[]{:S(2)}) async-start(), calls=%async_computation.10 | async-start | bytes 6553600 | tf_op jit(solution)/shard_map/all_gather | solution.py:212
  31.1 254.1 %all-to-all-start = ((bf16[4,512,2048]{2,1,0:T(8,128)(2,1)}), bf16[4,512,2048]{2,1,0:T(8,128)(2,1)}, u32[]{:S(2)}, u32[]{:S(2)}) async-start(bf16[4,512,2048]{2,1,0:T(8,128)(2,1)} %broadcast_in_dim.38), calls=%async_computation | async-start | bytes 16777216 | tf_op jit(solution)/shard_map/all_to_all | solution.py:227
  36.7 284.9 %reduce-scatter.7.cloned.1.call-start = ((), (), s32[]{:S(2)}) async-start(), calls=%async_computation.12 | async-start | bytes 5242880 | tf_op jit(solution)/shard_map/reduce_scatter | solution.py:277
  102.0 1.7 copy-start.5
  102.7 0.6 copy-start.2
  304.9 211.8 %all-to-all-start.1 = ((bf16[8,4,144,2048]{3,2,1,0:T(8,128)(2,1)}), bf16[8,4,144,2048]{3,2,1,0:T(8,128)(2,1)}, u32[]{:S(2)}, u32[]{:S(2)}) async-start(bf16[8,4,144,2048]{3,2,1,0:T(8,128)(2,1)} %pick_rows.3), calls=%async_computation.1 | async-start | bytes 37748736 | tf_op jit(solution)/shard_map/all_to_all | solution.py:253
  310.8 86.8 %copy-start.1 = (bf16[512,2048]{1,0:T(8,128)(2,1)S(1)}, bf16[512,2048]{1,0:T(8,128)(2,1)}, u32[]{:S(2)}) copy-start(bf16[512,2048]{1,0:T(8,128)(2,1)} %param.20) | copy-start | bytes 6291460
  310.8 86.7 %reduce-scatter.5.cloned.1.call-start = ((), (), s32[]{:S(2)}) async-start(), calls=%async_computation.11 | async-start | bytes 5242880 | tf_op jit(solution)/shard_map/reduce_scatter | solution.py:277
  321.2 195.4 %all-gather.9.cloned.1.call-start = ((), (), s32[]{:S(2)}) async-start(), calls=%async_computation.15 | async-start | bytes 5242880 | tf_op jit(solution)/shard_map/all_gather | solution.py:282
  527.2 109.7 %all-to-all-start.2 = ((bf16[8,4,144,1024]{3,2,1,0:T(8,128)(2,1)}), bf16[8,4,144,1024]{3,2,1,0:T(8,128)(2,1)}, u32[]{:S(2)}, u32[]{:S(2)}) async-start(bf16[8,4,144,1024]{3,2,1,0:T(8,128)(2,1)} %pick_rows.4), calls=%async_computation.3 | async-start | bytes 18874368 | tf_op jit(solution)/shard_map/all_to_all | solution.py:253
  532.2 82.3 %all-gather.11.cloned.1.call-start = ((), (), s32[]{:S(2)}) async-start(), calls=%async_computation.16 | async-start | bytes 5242880 | tf_op jit(solution)/shard_map/all_gather | solution.py:282
  636.9 109.7 %all-to-all-start.3 = ((bf16[8,4,144,1024]{3,2,1,0:T(8,128)(2,1)}), bf16[8,4,144,1024]{3,2,1,0:T(8,128)(2,1)}, u32[]{:S(2)}, u32[]{:S(2)}) async-start(bf16[8,4,144,1024]{3,2,1,0:T(8,128)(2,1)} %pick_rows.5), calls=%async_computation.5 | async-start | bytes 18874368 | tf_op jit(solution)/shard_map/all_to_all | solution.py:253
  641.9 36.9 %copy-start.7 = (bf16[1,768,2048]{2,1,0:T(8,128)(2,1)S(1)}, bf16[1,768,2048]{2,1,0:T(8,128)(2,1)}, u32[]{:S(2)}) copy-start(bf16[1,768,2048]{2,1,0:T(8,128)(2,1)} %param.25) | copy-start | bytes 9437188
  804.2 5.2 copy-start.3
  804.2 5.2 copy-start.4
  804.2 5.3 copy-start.6
  804.2 109.9 %all-to-all-start.5 = ((bf16[8,4,144,1024]{3,2,1,0:T(8,128)(2,1)}), bf16[8,4,144,1024]{3,2,1,0:T(8,128)(2,1)}, u32[]{:S(2)}, u32[]{:S(2)}) async-start(bf16[8,4,144,1024]{3,2,1,0:T(8,128)(2,1)} %bitcast.29), calls=%async_computation.8 | async-start | bytes 18874368 | tf_op jit(solution)/shard_map/all_to_all | solution.py:253
  914.1 109.8 %all-to-all-start.4 = ((bf16[8,4,144,1024]{3,2,1,0:T(8,128)(2,1)}), bf16[8,4,144,1024]{3,2,1,0:T(8,128)(2,1)}, u32[]{:S(2)}, u32[]{:S(2)}) async-start(bf16[8,4,144,1024]{3,2,1,0:T(8,128)(2,1)} %bitcast.28), calls=%async_computation.6 | async-start | bytes 18874368 | tf_op jit(solution)/shard_map/all_to_all | solution.py:253
  919.2 116.1 %reduce-scatter.11.cloned.1.call-start = ((), (), s32[]{:S(2)}) async-start(), calls=%async_computation.14 | async-start | bytes 5242880 | tf_op jit(solution)/shard_map/reduce_scatter | solution.py:310
  930.7 179.3 %reduce-scatter.9.cloned.1.call-start = ((), (), s32[]{:S(2)}) async-start(), calls=%async_computation.13 | async-start | bytes 5242880 | tf_op jit(solution)/shard_map/reduce_scatter | solution.py:310
Sparse Core Ops, SparseCore 0:
  10.2 64.0 all-gather.6
  102.1 156.5 reduce-scatter.6
  321.3 76.2 reduce-scatter.4
  401.7 81.2 all-gather.8
  534.3 80.1 all-gather.10
  930.8 76.1 reduce-scatter.10
  1035.4 74.5 reduce-scatter.8
